TPU v7x, 128 devices: a whole 4x4x4 slice. The times are simulated.
128 devices in a mesh: geom: 8 (over x, core), dom: 16 (over y, z).
Axes of the slice: x: 4, y: 4, z: 4, core: 2. Of those that a mesh axis runs over, the one named last changes fastest.
Arguments:
- h_in: bfloat16 [8, 8192, 512], P('geom', 'dom'), may hold values from -6 to 6
- edge_in: bfloat16 [8, 32768, 512], P('geom', 'dom'), may hold values from -6 to 6
- new_index: int32 [8, 8192], P('geom', 'dom'), may hold values from 0 to 8191, as said below
- source: int32 [8, 32768], P('geom', 'dom'), may hold values from 0 to 8191, as said below
- w_edge_in: bfloat16 [1536, 512], replicated, may hold values from -0.15625 to 0.15625
- w_edge_out: bfloat16 [512, 512], replicated, may hold values from -0.25 to 0.25
- w_node_in: bfloat16 [1024, 512], replicated, may hold values from -0.1875 to 0.1875
- w_node_out: bfloat16 [512, 512], replicated, may hold values from -0.25 to 0.25
- cot_nodes: bfloat16 [8, 8192, 512], P('geom', 'dom'), may hold values from -6 to 6
- cot_edges: bfloat16 [8, 32768, 512], P('geom', 'dom'), may hold values from -6 to 6
Outputs:
- node_new: bfloat16 [8, 8192, 512], P('geom', 'dom')
- edge_new: bfloat16 [8, 32768, 512], P('geom', 'dom')
- grad_in: bfloat16 [8, 8192, 512], P('geom', 'dom')
- grad_edge: bfloat16 [8, 32768, 512], P('geom', 'dom')
- weight_grads: float32 [3584, 512], P('dom')
Inputs may be any that keep to these rules, and one draw needn't show every extreme that they name: `new_index`: per geometry a permutation of the 8192 cells. The cells in rows k * 512 to (k + 1) * 512 - 1 of the old layout reach the rows of any one device of the new layout at most 48 times, exactly 48 times for some pairs. `source`: an edge of a cell in rows k * 512 to (k + 1) * 512 - 1 comes from a cell of the same range, of the last 64 cells of the range before, or of the first 64 cells of the range after.
All inputs are finite; a program needn't handle non-finite values.
Results may differ from a plain program's by a relative error of at most 0.019.
Values may be sent and summed in bfloat16 or wider, within the bound.
A program may use at most 128 MiB of HBM per device.

v0:
```python
import math

import jax
import jax.numpy as jnp
from jax import lax
from jax.sharding import PartitionSpec as P

HB = 64


def padded_2(cells, sides, width):
    for axis, dim in sides:
        count = lax.axis_size(axis)
        ends = count - 1
        head = lax.slice_in_dim(cells, 0, width, axis=dim)
        tail = lax.slice_in_dim(cells, cells.shape[dim] - width, cells.shape[dim], axis=dim)
        cells = jnp.concatenate(
            [
                lax.ppermute(tail, axis, [(i, (i + 1) % count) for i in range(ends)]),
                cells,
                lax.ppermute(head, axis, [((i + 1) % count, i) for i in range(ends)]),
            ],
            axis=dim,
        )
    return cells


def from_behind(value, axis, steps):
    count = lax.axis_size(axis)
    leading, last = (max(0, -steps), min(count, count - steps))
    return lax.ppermute(value, axis, [(source, source + steps) for source in range(leading, last)])


def normalize(values):
    center = values - jnp.mean(values, axis=-1, keepdims=True)
    inverse = lax.rsqrt(jnp.mean(center * center, axis=-1, keepdims=True) + 1e-05)
    return (center * inverse, inverse)


def normalize_back(normed, inverse, upstream):
    return inverse * (
        upstream
        - jnp.mean(upstream, axis=-1, keepdims=True)
        - normed * jnp.mean(upstream * normed, axis=-1, keepdims=True)
    )


def silu_slope(values):
    sigma = jax.nn.sigmoid(values)
    return sigma * (1.0 + values * (1.0 - sigma))


def matmul(left, right):
    return jnp.dot(left, right, preferred_element_type=jnp.float32)


def layer_math(
    nodes,
    edges,
    senders,
    w_edge_in,
    w_edge_out,
    w_node_in,
    w_node_out,
    cot_nodes,
    cot_edges,
    fan_in,
):
    width = nodes.shape[1]
    cell_count = nodes.shape[0]
    receivers = jnp.repeat(nodes, fan_in, axis=0)
    w_edge_self = w_edge_in[:width]
    w_edge_send = w_edge_in[width : 2 * width]
    w_edge_recv = w_edge_in[2 * width :]
    w_node_self = w_node_in[:width]
    w_node_agg = w_node_in[width:]
    edge_pre = (
        matmul(edges, w_edge_self) + matmul(senders, w_edge_send) + matmul(receivers, w_edge_recv)
    )
    edge_hidden = jax.nn.silu(edge_pre).astype(jnp.bfloat16)
    edge_post = matmul(edge_hidden, w_edge_out)
    edge_normed, edge_inverse = normalize(edge_post)
    edge_new = (edges.astype(jnp.float32) + edge_normed).astype(jnp.bfloat16)
    summed = jnp.sum(
        edge_new.astype(jnp.float32).reshape(cell_count, fan_in, width), axis=1
    ).astype(jnp.bfloat16)
    node_pre = matmul(nodes, w_node_self) + matmul(summed, w_node_agg)
    node_hidden = jax.nn.silu(node_pre).astype(jnp.bfloat16)
    node_post = matmul(node_hidden, w_node_out)
    node_normed, node_inverse = normalize(node_post)
    node_new = (nodes.astype(jnp.float32) + node_normed).astype(jnp.bfloat16)
    node_upstream = cot_nodes.astype(jnp.float32)
    node_post_grad = normalize_back(node_normed, node_inverse, node_upstream).astype(jnp.bfloat16)
    grad_node_out = matmul(node_hidden.T, node_post_grad)
    node_pre_grad = (matmul(node_post_grad, w_node_out.T) * silu_slope(node_pre)).astype(
        jnp.bfloat16
    )
    grad_node_self = matmul(nodes.T, node_pre_grad)
    grad_node_agg = matmul(summed.T, node_pre_grad)
    summed_grad = matmul(node_pre_grad, w_node_agg.T)
    edge_upstream = cot_edges.astype(jnp.float32) + jnp.repeat(summed_grad, fan_in, axis=0)
    edge_post_grad = normalize_back(edge_normed, edge_inverse, edge_upstream).astype(jnp.bfloat16)
    grad_edge_out = matmul(edge_hidden.T, edge_post_grad)
    edge_pre_grad = (matmul(edge_post_grad, w_edge_out.T) * silu_slope(edge_pre)).astype(
        jnp.bfloat16
    )
    grad_edge_self = matmul(edges.T, edge_pre_grad)
    grad_edge_send = matmul(senders.T, edge_pre_grad)
    grad_edge_recv = matmul(receivers.T, edge_pre_grad)
    grad_edge = (edge_upstream + matmul(edge_pre_grad, w_edge_self.T)).astype(jnp.bfloat16)
    sender_grad = matmul(edge_pre_grad, w_edge_send.T)
    receiver_grad = jnp.sum(
        matmul(edge_pre_grad, w_edge_recv.T).reshape(cell_count, fan_in, width), axis=1
    )
    node_grad = node_upstream + matmul(node_pre_grad, w_node_self.T) + receiver_grad
    stacked = jnp.concatenate(
        [
            grad_edge_self,
            grad_edge_send,
            grad_edge_recv,
            grad_edge_out,
            grad_node_self,
            grad_node_agg,
            grad_node_out,
        ],
        axis=0,
    )
    return (node_new, edge_new, grad_edge, node_grad, sender_grad, stacked)


def local(
    h_in,
    edge_in,
    new_index,
    source,
    w_edge_in,
    w_edge_out,
    w_node_in,
    w_node_out,
    cot_nodes,
    cot_edges,
):
    cell_count = h_in.shape[1]
    feature_width = h_in.shape[2]
    fan_in = source.shape[1] // cell_count
    part_count = lax.axis_size("dom")
    geom_count = lax.axis_size("geom")
    my_index = lax.axis_index("dom")
    rows_in = h_in[0]
    target = new_index[0]
    all_rows, all_ids = (
        lax.all_gather(rows_in, "dom", axis=0, tiled=True),
        lax.all_gather(target, "dom", axis=0, tiled=True),
    )
    mine = jnp.where(all_ids // cell_count == my_index, all_ids % cell_count, cell_count)
    nodes = jnp.zeros((cell_count, feature_width), jnp.bfloat16).at[mine].set(all_rows, mode="drop")
    padded = padded_2(nodes, (("dom", 0),), HB)
    local_rows = source[0] - my_index * cell_count + HB
    senders = padded[local_rows]
    node_new, edge_new, grad_edge, node_grad, sender_grad, stacked = layer_math(
        nodes,
        edge_in[0],
        senders,
        w_edge_in,
        w_edge_out,
        w_node_in,
        w_node_out,
        cot_nodes[0],
        cot_edges[0],
        fan_in,
    )
    padded_grad = (
        jnp.zeros((cell_count + 2 * HB, feature_width), jnp.float32).at[local_rows].add(sender_grad)
    )
    from_next = from_behind(padded_grad[:HB].astype(jnp.bfloat16), "dom", -1).astype(jnp.float32)
    from_prev = from_behind(padded_grad[cell_count + HB :].astype(jnp.bfloat16), "dom", 1).astype(
        jnp.float32
    )
    node_grad = node_grad + padded_grad[HB : HB + cell_count]
    node_grad = node_grad.at[cell_count - HB :].add(from_next).at[:HB].add(from_prev)
    grad_nodes = node_grad.astype(jnp.bfloat16)
    everything = lax.all_gather(grad_nodes, "dom", axis=0, tiled=True)
    grad_in = everything[target]
    scaled = stacked * (1.0 / math.sqrt(geom_count * part_count * cell_count * fan_in))
    partial_rows = lax.psum_scatter(
        scaled.astype(jnp.bfloat16), "dom", scatter_dimension=0, tiled=True
    )
    weight_grads = lax.psum(partial_rows, "geom").astype(jnp.float32)
    return (node_new[None], edge_new[None], grad_in[None], grad_edge[None], weight_grads)


def solution(mesh):
    return jax.shard_map(
        local,
        mesh=mesh,
        in_specs=(
            P("geom", "dom", None),
            P("geom", "dom", None),
            P("geom", "dom"),
            P("geom", "dom"),
            P(),
            P(),
            P(),
            P(),
            P("geom", "dom", None),
            P("geom", "dom", None),
        ),
        out_specs=(
            P("geom", "dom", None),
            P("geom", "dom", None),
            P("geom", "dom", None),
            P("geom", "dom", None),
            P("dom", None),
        ),
        check_vma=False,
    )
```

profile of v0, /device:TPU:1, one launch (start us, length us, event | category | flops | bytes accessed | tf_op | source)
XLA Modules:
  0.0 458.5 jit_solution(3349004230024600831)
XLA Ops:
  9.2 21.4 %all-gather = s32[1,8192]{1,0:T(1,128)S(1)} all-gather(s32[1,512]{1,0:T(1,128)} %param.16), channel_id=2, replica_groups=mesh['geom'=8,'dom'=16] {'dom'}, dimensions={1}, use_global_device_ids=true | all-gather | bytes 34816 | tf_op jit(solution)/shard_map/all_gather | solution.py:153
  31.5 4.9 %fusion.7 = f32[2048,512]{1,0:T(8,128)} fusion(bf16[1,2048,512]{2,1,0:T(8,128)(2,1)} %param.15, bf16[1536,512]{1,0:T(8,128)(2,1)} %param.18), kind=kOutput, calls=%fused_computation.24 | convolution fusion | flops 1073741824 | bytes 6815744 | tf_op jit(solution)/shard_map/dot_general | solution.py:54
  36.4 47.8 %all-gather.7.cloned.1.call-done = bf16[1,8192,512]{2,1,0:T(8,128)(2,1)} async-done(((bf16[1,512,512]{2,1,0:T(8,128)(2,1)}), bf16[1,8192,512]{2,1,0:T(8,128)(2,1)}) %all-gather.7.cloned.1.call-update) | async-done | bytes 8388624 | tf_op jit(solution)/shard_map/all_gather | solution.py:152
  84.3 35.9 %scatter_custom_fusion = bf16[512,512]{1,0:T(8,128)(2,1)S(1)} fusion(s32[8192]{0:T(1024)S(1)} %compare_select_fusion, bf16[1,8192,512]{2,1,0:T(8,128)(2,1)} %all-gather.7.cloned.1.call-done, bf16[]{:T(256)} %constant.109.clone.1), kind=kCustom, calls=%fused_computation.4 | custom fusion | bytes 8912898 | tf_op jit(solution)/shard_map/scatter | solution.py:156
  126.3 4.5 reshape.183
  130.8 5.0 %fusion.32 = f32[2048,512]{1,0:T(8,128)} fusion(bf16[2048,512]{1,0:T(8,128)(2,1)} %reshape.183, bf16[1536,512]{1,0:T(8,128)(2,1)} %param.18), kind=kOutput, calls=%fused_computation.62 | convolution fusion | flops 1073741824 | bytes 6815744 | tf_op jit(solution)/shard_map/dot_general | solution.py:54
  137.5 9.2 %gather_fusion = bf16[2048,512]{1,0:T(8,128)(2,1)} fusion(bf16[640,512]{1,0:T(8,128)(2,1)S(1)} %pad_maximum_fusion, s32[2048]{0:T(1024)S(1)} %broadcast_clamp_fusion), kind=kCustom, calls=%fused_computation | custom fusion | bytes 4202496 | tf_op jit(solution)/shard_map/gather | solution.py:159
  146.7 5.7 %add_add_fusion = f32[2048,512]{1,0:T(8,128)S(1)} fusion(f32[2048,512]{1,0:T(8,128)} %fusion.32, f32[2048,512]{1,0:T(8,128)} %fusion.7, bf16[2048,512]{1,0:T(8,128)(2,1)} %gather_fusion, bf16[1536,512]{1,0:T(8,128)(2,1)} %param.18), kind=kOutput, calls=%fused_computation.19 | convolution fusion | flops 1075838976 | bytes 15204352 | tf_op jit(solution)/shard_map/dot_general | solution.py:54
  160.8 4.0 reshape.184
  164.8 4.1 reduce.7
  179.4 5.5 %reshape.186 = f32[2048,512]{1,0:T(8,128)} reshape(f32[512,4,512]{2,1,0:T(4,128)} %broadcast_in_dim.47) | data formatting | bytes 8388608 | tf_op jit(solution)/shard_map/reshape | solution.py:101
  184.9 5.4 %broadcast_in_dim.48 = f32[1,2048,512]{2,1,0:T(8,128)} reshape(f32[512,4,512]{2,1,0:T(4,128)} %broadcast_in_dim.47) | data formatting | bytes 8388608 | tf_op jit(solution)/shard_map/broadcast_in_dim | solution.py:101
  212.3 4.3 fusion.34
  216.5 14.5 %scatter_custom_fusion.1 = f32[640,512]{1,0:T(8,128)} fusion(s32[2048]{0:T(1024)S(1)} %bitcast.89, f32[2048,512]{1,0:T(8,128)} %fusion.34, f32[]{:T(128)} %constant.120.clone.1), kind=kCustom, calls=%fused_computation.54 | custom fusion | flops 1048576 | bytes 1311232 | tf_op jit(solution)/shard_map/scatter-add | solution.py:173
  236.0 4.1 collective-permute-start.3
  241.3 4.3 fusion.30
  245.6 5.2 %reshape.187 = f32[512,4,512]{2,1,0:T(4,128)} reshape(f32[2048,512]{1,0:T(8,128)} %fusion.30) | data formatting | bytes 8388608 | tf_op jit(solution)/shard_map/reshape | solution.py:113
  250.9 5.8 %reduce_sum.99 = f32[512,512]{1,0:T(8,128)} reduce(f32[512,4,512]{2,1,0:T(4,128)} %reshape.187, f32[]{:T(128)} %constant.120.clone.1), dimensions={1}, to_apply=%region_10.11 | reduce | flops 786432 | bytes 5242884 | tf_op jit(solution)/shard_map/reduce_sum | solution.py:112
  264.5 27.7 %reduce-scatter.2.cloned.1.call-done = bf16[224,512]{1,0:T(8,128)(2,1)} async-done(((bf16[3584,512]{1,0:T(8,128)(2,1)}), bf16[224,512]{1,0:T(8,128)(2,1)}) %reduce-scatter.2.cloned.1.call-update) | async-done | bytes 229392 | tf_op jit(solution)/shard_map/reduce_scatter | solution.py:185
  298.5 5.7 %fusion.4 = bf16[1,2048,512]{2,1,0:T(8,128)(2,1)} fusion(bf16[2048,512]{1,0:T(8,128)(2,1)S(1)} %multiply_convert_fusion.1, f32[2048,512]{1,0:T(8,128)} %reshape.186, bf16[1,2048,512]{2,1,0:T(8,128)(2,1)} %param.23, bf16[1536,512]{1,0:T(8,128)(2,1)} %param.18), kind=kOutput, calls=%fused_computation.21 | convolution fusion | flops 1077936128 | bytes 11010048 | tf_op jit(solution)/shard_map/dot_general | solution.py:54
  304.1 49.1 %all-reduce.2.cloned.1.call-done = bf16[224,512]{1,0:T(8,128)(2,1)} async-done(((bf16[224,512]{1,0:T(8,128)(2,1)}), bf16[224,512]{1,0:T(8,128)(2,1)}) %all-reduce.2.cloned.1.call-update) | async-done | bytes 229392 | tf_op jit(solution)/shard_map/psum | solution.py:188
  354.9 77.6 %all-gather.5.cloned.1.call-done = bf16[8192,512]{0,1:T(8,128)(2,1)} async-done(((bf16[512,512]{0,1:T(8,128)(2,1)}), bf16[8192,512]{0,1:T(8,128)(2,1)}) %all-gather.5.cloned.1.call-update) | async-done | bytes 8388624 | tf_op jit(solution)/shard_map/all_gather | solution.py:182
  432.6 12.0 %copy.36 = bf16[8192,512]{1,0:T(8,128)(2,1)} copy(bf16[8192,512]{0,1:T(8,128)(2,1)} %all-gather.5.cloned.1.call-done) | data formatting | bytes 16777216 | tf_op jit(solution)/shard_map/all_gather | solution.py:182
  444.5 7.1 %gather_fusion.1 = bf16[512,512]{1,0:T(8,128)(2,1)} fusion(bf16[8192,512]{1,0:T(8,128)(2,1)} %copy.36, s32[1024]{0:T(1024)S(1)} %pad_clamp_fusion), kind=kCustom, calls=%fused_computation.1 | custom fusion | bytes 1050624 | tf_op jit(solution)/shard_map/gather | solution.py:183
  (127 shorter events, 73.2 us)
Async XLA Ops:
  7.2 147.2 %copy-start = (bf16[512,512]{1,0:T(8,128)(2,1)S(1)}, bf16[512,512]{1,0:T(8,128)(2,1)}, u32[]{:S(2)}) copy-start(bf16[512,512]{1,0:T(8,128)(2,1)} %param.19) | copy-start | bytes 1572868
  7.2 77.1 %all-gather.7.cloned.1.call-start = ((), (), s32[]{:S(2)}) async-start(), calls=%async_computation.4 | async-start | bytes 8912896 | tf_op jit(solution)/shard_map/all_gather | solution.py:152
  7.9 284.3 %reduce-scatter.2.cloned.1.call-start = ((), (), s32[]{:S(2)}) async-start(), calls=%async_computation.2 | async-start | bytes 3899392 | tf_op jit(solution)/shard_map/reduce_scatter | solution.py:185
  9.2 164.3 %copy-start.6 = (bf16[1,512,512]{1,2,0:T(8,128)(2,1)}, bf16[1,512,512]{1,2,0:T(8,128)(2,1)S(1)}, u32[]{:S(2)}) copy-start(bf16[1,512,512]{1,2,0:T(8,128)(2,1)S(1)} %copy.31) | copy-start | bytes 1572868
  120.2 17.3 %collective-permute-start = (bf16[64,512]{1,0:T(8,128)(2,1)S(1)}, bf16[64,512]{1,0:T(8,128)(2,1)S(1)}, u32[]{:S(2)}, u32[]{:S(2)}) collective-permute-start(bf16[64,512]{1,0:T(8,128)(2,1)S(1)} %get-tuple-element.48), channel_id=1, source_target_pairs={{0,1},{1,2},{2,3},{3,4},{4,5},{5,6},{6,7},{7,8},{8,9},{9,10},{10,1... | collective-permute-start | bytes 196616 | tf_op jit(solution)/shard_map/ppermute | solution.py:19
  123.2 14.3 %collective-permute-start.1 = (bf16[64,512]{1,0:T(8,128)(2,1)S(1)}, bf16[64,512]{1,0:T(8,128)(2,1)S(1)}, u32[]{:S(2)}, u32[]{:S(2)}) collective-permute-start(bf16[64,512]{1,0:T(8,128)(2,1)S(1)} %get-tuple-element.49), channel_id=1, source_target_pairs={{1,0},{2,1},{3,2},{4,3},{5,4},{6,5},{7,6},{8,7},{9,8},{10,9},{11,1... | collective-permute-start | bytes 196616 | tf_op jit(solution)/shard_map/ppermute | solution.py:21
  130.8 5.0 %copy-start.18 = (bf16[1024,512]{1,0:T(8,128)(2,1)S(1)}, bf16[1024,512]{1,0:T(8,128)(2,1)}, u32[]{:S(2)}) copy-start(bf16[1024,512]{1,0:T(8,128)(2,1)} %param.20) | copy-start | bytes 3145732
  155.9 3.1 copy-start.9
  169.0 4.1 copy-start.16
  171.0 3.7 copy-start.23
  184.9 5.4 %copy-start.5 = (bf16[1,2048,512]{2,1,0:T(8,128)(2,1)S(1)}, bf16[1,2048,512]{2,1,0:T(8,128)(2,1)}, u32[]{:S(2)}) copy-start(bf16[1,2048,512]{2,1,0:T(8,128)(2,1)} %param.23) | copy-start | bytes 6291460
  190.4 3.4 copy-start.2
  193.8 3.4 copy-start.4
  197.3 2.2 copy-start.21
  199.4 2.3 copy-start.10
  212.2 141.0 %all-reduce.2.cloned.1.call-start = ((), (), s32[]{:S(2)}) async-start(), calls=%async_computation.3 | async-start | bytes 458752 | tf_op jit(solution)/shard_map/psum | solution.py:188
  236.0 56.3 %collective-permute-start.3 = (bf16[64,512]{0,1:T(8,128)(2,1)S(1)}, bf16[64,512]{0,1:T(8,128)(2,1)S(1)}, u32[]{:S(2)}, u32[]{:S(2)}) collective-permute-start(bf16[64,512]{0,1:T(8,128)(2,1)S(1)} %get-tuple-element.46), channel_id=1, source_target_pairs={{0,1},{1,2},{2,3},{3,4},{4,5},{5,6},{6,7},{7,8},{8,9},{9,10},{10,1... | collective-permute-start | bytes 196616 | tf_op jit(solution)/shard_map/ppermute | solution.py:31
  240.0 21.5 %collective-permute-start.2 = (bf16[64,512]{0,1:T(8,128)(2,1)}, bf16[64,512]{0,1:T(8,128)(2,1)S(1)}, u32[]{:S(2)}, u32[]{:S(2)}) collective-permute-start(bf16[64,512]{0,1:T(8,128)(2,1)} %get-tuple-element.47), channel_id=1, source_target_pairs={{1,0},{2,1},{3,2},{4,3},{5,4},{6,5},{7,6},{8,7},{9,8},{10,9},{11,1... | collective-permute-start | bytes 196616 | tf_op jit(solution)/shard_map/ppermute | solution.py:31
  250.9 8.3 %copy-start.7 = (bf16[1,512,512]{1,2,0:T(8,128)(2,1)S(1)}, bf16[1,512,512]{1,2,0:T(8,128)(2,1)}, u32[]{:S(2)}) copy-start(bf16[1,512,512]{1,2,0:T(8,128)(2,1)} %copy-done.6) | copy-start | bytes 1572868
  250.9 8.3 %copy-start.13 = (bf16[512,512]{1,0:T(8,128)(2,1)S(1)}, bf16[512,512]{1,0:T(8,128)(2,1)}, u32[]{:S(2)}) copy-start(bf16[512,512]{1,0:T(8,128)(2,1)} %copy-done.11) | copy-start | bytes 1572868
  259.2 38.2 %copy-start.27 = (s32[1,512]{1,0:T(1,128)S(1)}, s32[1,512]{1,0:T(1,128)}, u32[]{:S(2)}) copy-start(s32[1,512]{1,0:T(1,128)} %param.16) | copy-start | bytes 6148
  261.5 36.0 %copy-start.22 = (bf16[1,512,512]{1,2,0:T(8,128)(2,1)S(1)}, bf16[1,512,512]{1,2,0:T(8,128)(2,1)}, u32[]{:S(2)}) copy-start(bf16[1,512,512]{1,2,0:T(8,128)(2,1)} %get-tuple-element.45) | copy-start | bytes 1572868
  292.2 140.4 %all-gather.5.cloned.1.call-start = ((), (), s32[]{:S(2)}) async-start(), calls=%async_computation.1 | async-start | bytes 8912896 | tf_op jit(solution)/shard_map/all_gather | solution.py:182
  432.6 19.1 %copy-start.1 = (bf16[512,512]{1,0:T(8,128)(2,1)S(1)}, bf16[512,512]{1,0:T(8,128)(2,1)}, u32[]{:S(2)}) copy-start(bf16[512,512]{1,0:T(8,128)(2,1)} %param.19) | copy-start | bytes 1572868
  (13 other events, 18.9 us)
Sparse Core Ops, SparseCore 0:
  10.1 74.0 all-gather.6
  212.3 79.7 reduce-scatter.1
  294.5 58.6 all-reduce.1
  355.2 77.3 all-gather.4
where the time goes:
time: 465 us; the launch traced here: 458 us
  waiting for transfers between devices  203 us (44%)
  local copies, waits for them, and re-layouts  115 us (25%)
  matrix products  49 us (11%)
  other arithmetic  46.3 us (10%)
  blocking collectives  21.4 us (5%)
  between operations  14.5 us (3%)
  starting transfers between devices  9.77 us (2%)
    all_gather x1, waiting for transfers between devices, local(): everything = lax.all_gather(grad_nodes, 'dom', axis=0, tiled=True)  77.6 us
    psum x1, waiting for transfers between devices, local(): weight_grads = lax.psum(partial_rows, 'geom').astype(jnp.float32)  49.1 us
    dot_general x21, matrix products, matmul(): return jnp.dot(left, right, preferred_element_type=jnp.float32)  49 us
    all_gather x1, waiting for transfers between devices, local(): lax.all_gather(rows_in, 'dom', axis=0, tiled=True)  47.8 us
    scatter x2, local copies, waits for them, and re-layouts, local(): jnp.zeros((cell_count, feature_width), jnp.bfloat16).at[mine]  36.1 us
    reduce_scatter x1, waiting for transfers between devices, local(): lax.psum_scatter(scaled.astype(jnp.bfloat16), 'dom', scatter_dimension=0,...  27.7 us
    all_gather x1, blocking collectives, local(): lax.all_gather(target, 'dom', axis=0, tiled=True)  21.4 us
    scatter-add x1, other arithmetic, local(): jnp.zeros((cell_count + 2 * HB, feature_width), jnp.float32).at[local_rows]  14.5 us
  transfers between devices with their start and end apart: 8, of which 4 were waited for; matrix products, arithmetic and copies ran while one was open for 17% of the time, Pallas kernels for 0%

commit v1 on v0

v1 whole, which is shorter than its diff:
```python
import functools
import math

import jax
import jax.numpy as jnp
from jax import lax
from jax.experimental import pallas as pl
from jax.experimental.pallas import tpu as pltpu
from jax.sharding import PartitionSpec as P

MESH = pl.DeviceIdType.MESH
BF = jnp.bfloat16
F32 = jnp.float32

D = 512
K = 4
C = 512
HB = 64
PADDED = C + 2 * HB
NP = 16
CAP = 48
SLOTS = NP * CAP
TC = 128
TE = TC * K
TILES = C // TC
SEL = PADDED + TC
RC = 64
SQUARES = 7
PER_DOM = SQUARES * D // NP
PER_CORE = PER_DOM // 2


def nn(a, b):
    return jnp.dot(a, b, preferred_element_type=F32)


def nt(a, b):
    return lax.dot_general(a, b, (((1,), (1,)), ((), ())), preferred_element_type=F32)


def tn(a, b):
    return lax.dot_general(a, b, (((0,), (0,)), ((), ())), preferred_element_type=F32)


def sigmoid(v):
    return 0.5 * jnp.tanh(0.5 * v) + 0.5


def iota(shape, dim):
    return lax.broadcasted_iota(jnp.int32, shape, dim)


def remote(src, dst, send, recv, geom, dom):
    return pltpu.make_async_remote_copy(
        src_ref=src,
        dst_ref=dst,
        send_sem=send,
        recv_sem=recv,
        device_id=(geom, dom),
        device_id_type=MESH,
    )


def signal(sem, geom, dom):
    pl.semaphore_signal(sem, inc=1, device_id=(geom, dom), device_id_type=MESH)


def pack_matrix(slot):
    return (iota((SLOTS, C), 0) == slot).astype(BF)


def unpack_blocks(ids):
    turned = ids.T
    lanes = iota((CAP, C), 1).astype(F32)
    return [(turned[0:CAP, p : p + 1] == lanes).astype(BF) for p in range(NP)]


def deliver_kernel(
    h_ref, tgt_ref, pad_ref, ids_ref, slot_ref,
    sbuf, rbuf, sids, rids, edge_out, edge_in, mt,
    send, recv, isend, irecv, hsend, hrecv,
):
    geom = lax.axis_index("geom")
    me = lax.axis_index("dom")
    barrier = pltpu.get_barrier_semaphore()
    for p in range(1, NP):
        signal(barrier, geom, (me + p) % NP)

    tgt = tgt_ref[...]
    off = ((tgt >> 9) - me) & (NP - 1)
    row = tgt & (C - 1)
    owned = (iota((NP, C), 0) == off).astype(F32)
    upper = (iota((C, C), 0) < iota((C, C), 1)).astype(BF)
    before = nn(owned.astype(BF), upper)
    rank = jnp.sum(owned * before, axis=0, keepdims=True).astype(jnp.int32)
    slot = off * CAP + rank
    slot_ref[...] = slot
    ranked = (iota((128, C), 0) == rank).astype(BF)
    high = (row >> 5).astype(F32)
    low = (row & 31).astype(F32)
    coded = nt(jnp.concatenate([owned * high, owned * low, owned], axis=0).astype(BF), ranked)
    ids = 32.0 * coded[0:NP] + coded[NP : 2 * NP] + coded[2 * NP :] - 1.0
    for p in range(NP):
        sids[p] = jnp.broadcast_to(ids[p : p + 1, :], (8, 128))
    packed = nn(pack_matrix(slot), h_ref[...]).astype(BF)
    sbuf[...] = packed.reshape(NP, CAP, D)
    rbuf[0] = packed[0:CAP]

    pl.semaphore_wait(barrier, NP - 1)
    copies = []
    for p in range(1, NP):
        peer = (me + p) % NP
        copies.append(remote(sids.at[p], rids.at[p], isend.at[p], irecv.at[p], geom, peer))
        copies.append(remote(sbuf.at[p], rbuf.at[p], send.at[p], recv.at[p], geom, peer))
    for copy in copies:
        copy.start()
    for copy in copies[0::2]:
        copy.wait_recv()
    got = jnp.concatenate([ids[0:1]] + [rids[p, 0:1, :] for p in range(1, NP)], axis=0)
    ids_ref[...] = got
    for p, block in enumerate(unpack_blocks(got)):
        mt[pl.ds(p * CAP, CAP), :] = block
    for copy in copies[1::2]:
        copy.wait_recv()
    nodes = tn(mt[...], rbuf[...].reshape(SLOTS, D)).astype(BF)
    edge_out[0] = nodes[0:HB]
    edge_out[1] = nodes[C - HB : C]
    to_prev = remote(edge_out.at[0], edge_in.at[1], hsend.at[0], hrecv.at[1], geom, (me + NP - 1) % NP)
    to_next = remote(edge_out.at[1], edge_in.at[0], hsend.at[1], hrecv.at[0], geom, (me + 1) % NP)
    to_prev.start()
    to_next.start()
    pad_ref[HB : HB + C, :] = nodes
    to_prev.wait_recv()
    to_next.wait_recv()
    pad_ref[0:HB, :] = edge_in[0]
    pad_ref[HB + C :, :] = edge_in[1]
    for copy in copies:
        copy.wait_send()
    to_prev.wait_send()
    to_next.wait_send()


def deliver(h, tgt):
    vm = pl.BlockSpec(memory_space=pltpu.VMEM)
    return pl.pallas_call(
        deliver_kernel,
        out_shape=(
            jax.ShapeDtypeStruct((PADDED, D), BF),
            jax.ShapeDtypeStruct((NP, 128), F32),
            jax.ShapeDtypeStruct((1, C), jnp.int32),
        ),
        in_specs=[vm, vm],
        out_specs=(vm, vm, vm),
        scratch_shapes=[
            pltpu.VMEM((NP, CAP, D), BF),
            pltpu.VMEM((NP, CAP, D), BF),
            pltpu.VMEM((NP, 8, 128), F32),
            pltpu.VMEM((NP, 8, 128), F32),
            pltpu.VMEM((2, HB, D), BF),
            pltpu.VMEM((2, HB, D), BF),
            pltpu.VMEM((SLOTS, C), BF),
        ]
        + [pltpu.SemaphoreType.DMA((NP,))] * 4
        + [pltpu.SemaphoreType.DMA((2,))] * 2,
        compiler_params=pltpu.CompilerParams(collective_id=0, has_side_effects=True),
        name="deliver",
    )(h, tgt)


def layer_kernel(
    pad_ref, src_ref, edges_ref, cotn_ref, cote_ref, wei_ref, weo_ref, wni_ref, wno_ref,
    edge_new_ref, node_new_ref, grad_edge_ref, ng_ref, halo_ref, w_ref,
    sel, sel_t, comb, spread, gather4,
    big, slope, hid, normed, inv, ups, post_grad, pre_grad,
    total, acc,
):
    step = pl.program_id(0)
    me = lax.axis_index("dom")
    w_self, w_send, w_recv = wei_ref.at[0:D], wei_ref.at[D : 2 * D], wei_ref.at[2 * D : 3 * D]
    w_nself, w_nagg = wni_ref.at[0:D], wni_ref.at[D : 2 * D]
    rows = pl.ds(pl.multiple_of(step * TC, TC), TC)

    @pl.when(step == 0)
    def _():
        comb[0:PADDED, :] = nn(pad_ref[...], w_send[...]).astype(BF)
        sel[:, PADDED:] = (iota((TE, TC), 0) // K == iota((TE, TC), 1)).astype(BF)
        sel_t[PADDED:, :] = (iota((TC, TE), 1) // K == iota((TC, TE), 0)).astype(BF)
        total[...] = jnp.zeros_like(total)
        acc[...] = jnp.zeros_like(acc)

    nodes = pad_ref[pl.ds(pl.multiple_of(HB + step * TC, HB), TC), :]
    edges = edges_ref[...]
    src = src_ref[...] - (me * C - HB)
    sel_t[0:PADDED, :] = (iota((PADDED, TE), 0) == src).astype(BF)
    src_col = jnp.broadcast_to(src.astype(F32), (128, TE)).T.astype(jnp.int32)
    for b in range(PADDED // 128):
        sel[:, b * 128 : (b + 1) * 128] = (src_col == iota((TE, 128), 1) + b * 128).astype(BF)
    comb[PADDED:, :] = nn(nodes, w_recv[...]).astype(BF)

    big[...] = nn(edges, w_self[...]) + nn(sel[...], comb[...])
    for r in range(0, TE, RC):
        v = big[r : r + RC, :]
        s = sigmoid(v)
        h = v * s
        hid[r : r + RC, :] = h.astype(BF)
        slope[r : r + RC, :] = s + h * (1.0 - s)
    big[...] = nn(hid[...], weo_ref[...])
    for r in range(0, TE, RC):
        v = big[r : r + RC, :]
        center = v - jnp.mean(v, axis=-1, keepdims=True)
        i = lax.rsqrt(jnp.mean(center * center, axis=-1, keepdims=True) + 1e-05)
        n = center * i
        normed[r : r + RC, :] = n
        inv[r : r + RC, :] = jnp.broadcast_to(i, (RC, 128))
        edge_new_ref[r : r + RC, :] = (edges_ref[r : r + RC, :].astype(F32) + n).astype(BF)

    four = sel_t[PADDED:, :]
    summed = nn(four, edge_new_ref[...]).astype(BF)
    v = nn(nodes, w_nself[...]) + nn(summed, w_nagg[...])
    s = sigmoid(v)
    h = v * s
    node_slope = s + h * (1.0 - s)
    node_hid = h.astype(BF)
    v = nn(node_hid, wno_ref[...])
    center = v - jnp.mean(v, axis=-1, keepdims=True)
    i = lax.rsqrt(jnp.mean(center * center, axis=-1, keepdims=True) + 1e-05)
    n = center * i
    node_new_ref[...] = (nodes.astype(F32) + n).astype(BF)
    u = cotn_ref[...].astype(F32)
    m1 = jnp.mean(u, axis=-1, keepdims=True)
    m2 = jnp.mean(u * n, axis=-1, keepdims=True)
    node_post_grad = (i * (u - m1 - n * m2)).astype(BF)
    node_pre_grad = (nt(node_post_grad, wno_ref[...]) * node_slope).astype(BF)
    spread_grad = nt(node_pre_grad, w_nagg[...]).astype(BF)

    ups[...] = nn(sel[:, PADDED:], spread_grad)
    for r in range(0, TE, RC):
        u = cote_ref[r : r + RC, :].astype(F32) + ups[r : r + RC, :]
        ups[r : r + RC, :] = u
        n = normed[r : r + RC, :]
        m1 = jnp.mean(u, axis=-1, keepdims=True)
        m2 = jnp.mean(u * n, axis=-1, keepdims=True)
        post_grad[r : r + RC, :] = (inv[r : r + RC, 0:1] * (u - m1 - n * m2)).astype(BF)
    big[...] = nt(post_grad[...], weo_ref[...])
    for r in range(0, TE, RC):
        pre_grad[r : r + RC, :] = (big[r : r + RC, :] * slope[r : r + RC, :]).astype(BF)
    g = pre_grad[...]
    big[...] = nt(g, w_self[...])
    for r in range(0, TE, RC):
        grad_edge_ref[r : r + RC, :] = (ups[r : r + RC, :] + big[r : r + RC, :]).astype(BF)
    total[...] += nn(sel_t[0:PADDED, :], g)
    recv_grad = nn(four, g).astype(BF)
    ng_ref[rows, :] = (
        cotn_ref[...].astype(F32) + nt(node_pre_grad, w_nself[...]) + nt(recv_grad, w_recv[...])
    )
    acc[0:D, :] += tn(edges, g)
    acc[2 * D : 3 * D, :] += tn(nodes, recv_grad)
    acc[3 * D : 4 * D, :] += tn(hid[...], post_grad[...])
    acc[4 * D : 5 * D, :] += tn(nodes, node_pre_grad)
    acc[5 * D : 6 * D, :] += tn(summed, node_pre_grad)
    acc[6 * D : 7 * D, :] += tn(node_hid, node_post_grad)

    @pl.when(step == TILES - 1)
    def _():
        scale = 1.0 / math.sqrt(8 * NP * C * K)
        t = total[...].astype(BF)
        acc[D : 2 * D, :] = tn(pad_ref[...], t)
        back = nt(t, w_send[...])
        ng_ref[...] += back[HB : HB + C]
        halo_ref[0] = back[0:HB].astype(BF)
        halo_ref[1] = back[HB + C :].astype(BF)
        w_ref[...] = (acc[...] * scale).astype(BF)


def layer(padded, source, edges, cot_nodes, cot_edges, wei, weo, wni, wno):
    def whole(shape):
        return pl.BlockSpec(shape, lambda i: (0,) * len(shape), pipeline_mode=pl.Buffered(1))

    def tile(rows):
        return pl.BlockSpec((rows, D), lambda i: (i, 0))

    return pl.pallas_call(
        layer_kernel,
        grid=(TILES,),
        out_shape=(
            jax.ShapeDtypeStruct((C * K, D), BF),
            jax.ShapeDtypeStruct((C, D), BF),
            jax.ShapeDtypeStruct((C * K, D), BF),
            jax.ShapeDtypeStruct((C, D), F32),
            jax.ShapeDtypeStruct((2, HB, D), BF),
            jax.ShapeDtypeStruct((SQUARES * D, D), BF),
        ),
        in_specs=[
            whole((PADDED, D)),
            pl.BlockSpec((1, TE), lambda i: (0, i)),
            tile(TE),
            tile(TC),
            tile(TE),
            whole((3 * D, D)),
            whole((D, D)),
            whole((2 * D, D)),
            whole((D, D)),
        ],
        out_specs=(
            tile(TE),
            tile(TC),
            tile(TE),
            whole((C, D)),
            whole((2, HB, D)),
            whole((SQUARES * D, D)),
        ),
        scratch_shapes=[
            pltpu.VMEM((TE, SEL), BF),
            pltpu.VMEM((SEL, TE), BF),
            pltpu.VMEM((SEL, D), BF),
            pltpu.VMEM((8, 128), BF),
            pltpu.VMEM((8, 128), BF),
            pltpu.VMEM((TE, D), F32),
            pltpu.VMEM((TE, D), F32),
            pltpu.VMEM((TE, D), BF),
            pltpu.VMEM((TE, D), F32),
            pltpu.VMEM((TE, 128), F32),
            pltpu.VMEM((TE, D), F32),
            pltpu.VMEM((TE, D), BF),
            pltpu.VMEM((TE, D), BF),
            pltpu.VMEM((PADDED, D), F32),
            pltpu.VMEM((SQUARES * D, D), F32),
        ],
        compiler_params=pltpu.CompilerParams(vmem_limit_bytes=60 * 1024 * 1024),
        name="layer",
    )(padded, source, edges, cot_nodes, cot_edges, wei, weo, wni, wno)


def collect_kernel(
    ng_ref, halo_ref, w_ref, ids_ref, slot_ref, grad_ref, out_ref,
    hbuf, sback, rback, pbuf, wsum, r1a, r1b, p1a, p1b, r2a, r2b, r3, fin,
    hsend, hrecv, bsend, brecv, psend, precv, s1a, v1a, s1b, v1b,
    s2a, v2a, s2b, v2b, s3, v3, s4, v4,
):
    geom = lax.axis_index("geom")
    me = lax.axis_index("dom")
    core = geom % 2
    x = geom // 2
    y = me // 4
    z = me % 4
    partner = x * 2 + (1 - core)
    barrier = pltpu.get_barrier_semaphore()
    signal(barrier, partner, me)
    for p in range(1, NP):
        signal(barrier, geom, (me + p) % NP)
    for d in range(1, 4):
        signal(barrier, ((x + d) % 4) * 2 + core, me)
    pl.semaphore_wait(barrier, NP + 3)

    to_prev = remote(halo_ref.at[0], hbuf.at[1], hsend.at[0], hrecv.at[1], geom, (me + NP - 1) % NP)
    to_next = remote(halo_ref.at[1], hbuf.at[0], hsend.at[1], hrecv.at[0], geom, (me + 1) % NP)
    to_prev.start()
    to_next.start()
    pair = [
        remote(w_ref.at[i, :, 1 - core], pbuf.at[i], psend.at[i], precv.at[i], partner, me)
        for i in range(4)
    ]
    for copy in pair:
        copy.start()

    blocks = unpack_blocks(ids_ref[...])
    to_prev.wait_recv()
    to_next.wait_recv()
    first = ng_ref[0:HB, :] + hbuf[0].astype(F32)
    last = ng_ref[C - HB :, :] + hbuf[1].astype(F32)
    cells = jnp.concatenate([first, ng_ref[HB : C - HB, :], last], axis=0).astype(BF)
    packed = nn(jnp.concatenate(blocks, axis=0), cells).astype(BF)
    sback[...] = packed.reshape(NP, CAP, D)
    rback[0] = packed[0:CAP]
    backs = [
        remote(sback.at[p], rback.at[p], bsend.at[p], brecv.at[p], geom, (me + NP - p) % NP)
        for p in range(1, NP)
    ]
    for copy in backs:
        copy.start()

    for i in range(4):
        pair[i].wait_recv()
        for j in range(4):
            mine = w_ref[i, j, pl.ds(core, 1)].reshape(PER_CORE, D)
            wsum[i, j] = (mine.astype(F32) + pbuf[i, j].astype(F32)).astype(BF)

    half = D // 2
    ones = []
    for d in range(1, 4):
        ty, tz = (y + d) % 4, (z + d) % 4
        ones.append(
            remote(wsum.at[ty, :, :, 0:half], r1a.at[d - 1], s1a.at[d - 1], v1a.at[d - 1], geom, ty * 4 + z)
        )
        ones.append(
            remote(wsum.at[:, tz, :, half:D], r1b.at[d - 1], s1b.at[d - 1], v1b.at[d - 1], geom, y * 4 + tz)
        )
    for copy in ones:
        copy.start()

    for copy in backs:
        copy.wait_recv()
    grad_ref[...] = tn(pack_matrix(slot_ref[...]), rback[...].reshape(SLOTS, D)).astype(BF)

    for copy in ones:
        copy.wait_recv()
    for j in range(4):
        own = wsum[pl.ds(y, 1), j, :, 0:half].reshape(PER_CORE, half).astype(F32)
        for d in range(3):
            own += r1a[d, j].astype(F32)
        p1a[j] = own.astype(BF)
        own = wsum[j, pl.ds(z, 1), :, half:D].reshape(PER_CORE, half).astype(F32)
        for d in range(3):
            own += r1b[d, j].astype(F32)
        p1b[j] = own.astype(BF)
    twos = []
    for d in range(1, 4):
        ty, tz = (y + d) % 4, (z + d) % 4
        twos.append(remote(p1a.at[tz], r2a.at[d - 1], s2a.at[d - 1], v2a.at[d - 1], geom, y * 4 + tz))
        twos.append(remote(p1b.at[ty], r2b.at[d - 1], s2b.at[d - 1], v2b.at[d - 1], geom, ty * 4 + z))
    for copy in twos:
        copy.start()
    for copy in twos:
        copy.wait_recv()
    left = p1a[pl.ds(z, 1)].reshape(PER_CORE, half).astype(F32)
    right = p1b[pl.ds(y, 1)].reshape(PER_CORE, half).astype(F32)
    for d in range(3):
        left += r2a[d].astype(F32)
        right += r2b[d].astype(F32)
    r3[pl.ds(x, 1)] = jnp.concatenate([left, right], axis=1).astype(BF).reshape(1, PER_CORE, D)
    threes = [
        remote(r3.at[x], r3.at[x], s3.at[d - 1], v3.at[d - 1], ((x + d) % 4) * 2 + core, me)
        for d in range(1, 4)
    ]
    for copy in threes:
        copy.start()
    for d in range(1, 4):
        source = (x + 4 - d) % 4
        remote(r3.at[x], r3.at[source], s3.at[d - 1], v3.at[d - 1], source * 2 + core, me).wait_recv()
    done = r3[0].astype(F32) + r3[1].astype(F32) + r3[2].astype(F32) + r3[3].astype(F32)
    fin[pl.ds(core, 1)] = done.reshape(1, PER_CORE, D)
    four = remote(fin.at[core], fin.at[core], s4, v4, partner, me)
    four.start()
    remote(fin.at[core], fin.at[1 - core], s4, v4, partner, me).wait_recv()
    out_ref[...] = fin[...].reshape(PER_DOM, D)
    for copy in [to_prev, to_next] + pair + backs + ones + twos + threes + [four]:
        copy.wait_send()


def collect(ng, halo, w, ids, slot):
    vm = pl.BlockSpec(memory_space=pltpu.VMEM)
    half = D // 2
    dma = pltpu.SemaphoreType.DMA
    return pl.pallas_call(
        collect_kernel,
        out_shape=(
            jax.ShapeDtypeStruct((C, D), BF),
            jax.ShapeDtypeStruct((PER_DOM, D), F32),
        ),
        in_specs=[vm] * 5,
        out_specs=(vm, vm),
        scratch_shapes=[
            pltpu.VMEM((2, HB, D), BF),
            pltpu.VMEM((NP, CAP, D), BF),
            pltpu.VMEM((NP, CAP, D), BF),
            pltpu.VMEM((4, 4, PER_CORE, D), BF),
            pltpu.VMEM((4, 4, PER_CORE, D), BF),
            pltpu.VMEM((3, 4, PER_CORE, half), BF),
            pltpu.VMEM((3, 4, PER_CORE, half), BF),
            pltpu.VMEM((4, PER_CORE, half), BF),
            pltpu.VMEM((4, PER_CORE, half), BF),
            pltpu.VMEM((3, PER_CORE, half), BF),
            pltpu.VMEM((3, PER_CORE, half), BF),
            pltpu.VMEM((4, PER_CORE, D), BF),
            pltpu.VMEM((2, PER_CORE, D), F32),
            dma((2,)), dma((2,)), dma((NP,)), dma((NP,)), dma((4,)), dma((4,)),
            dma((3,)), dma((3,)), dma((3,)), dma((3,)),
            dma((3,)), dma((3,)), dma((3,)), dma((3,)),
            dma((3,)), dma((3,)), dma, dma,
        ],
        compiler_params=pltpu.CompilerParams(collective_id=1, has_side_effects=True),
        name="collect",
    )(ng, halo, w, ids, slot)


def local(
    h_in, edge_in, new_index, source, w_edge_in, w_edge_out, w_node_in, w_node_out, cot_nodes, cot_edges
):
    padded, ids, slot = deliver(h_in[0], new_index)
    edge_new, node_new, grad_edge, ng, halo, w = layer(
        padded, source, edge_in[0], cot_nodes[0], cot_edges[0], w_edge_in, w_edge_out, w_node_in, w_node_out
    )
    grad_in, weight_grads = collect(ng, halo, w.reshape(4, 4, 2, PER_CORE, D), ids, slot)
    return (node_new[None], edge_new[None], grad_in[None], grad_edge[None], weight_grads)


def solution(mesh):
    return jax.shard_map(
        local,
        mesh=mesh,
        in_specs=(
            P("geom", "dom", None),
            P("geom", "dom", None),
            P("geom", "dom"),
            P("geom", "dom"),
            P(),
            P(),
            P(),
            P(),
            P("geom", "dom", None),
            P("geom", "dom", None),
        ),
        out_specs=(
            P("geom", "dom", None),
            P("geom", "dom", None),
            P("geom", "dom", None),
            P("geom", "dom", None),
            P("dom", None),
        ),
        check_vma=False,
    )
```

time: 465 us -> 110 us (0.24); the launches traced: 458 us -> 110 us
  waiting for transfers between devices: 203 us -> 0 us
  local copies, waits for them, and re-layouts: 115 us -> 3.68 us
  Pallas kernels: 0 us -> 105 us
  matrix products: 49 us -> 0 us
  other arithmetic: 46.3 us -> 0 us
  blocking collectives: 21.4 us -> 0 us
  between operations: 14.5 us -> 0.65 us
  starting transfers between devices: 9.77 us -> 0 us
    all_gather x2 -> x0, waiting for transfers between devices: 125 us -> none  [the longest x1 77.6 us: local(): everything = lax.all_gather(grad_nodes, 'dom', axis=0, tiled=True)]
    pallas_call x0 -> x3, Pallas kernels: none -> 105 us  [the longest x1 45.9 us: collect(): pl.pallas_call(collect_kernel, out_shape=(jax.ShapeDtypeStruct((C, D), BF...]
    psum x1 -> x0, waiting for transfers between devices: 49.1 us -> none  [local(): weight_grads = lax.psum(partial_rows, 'geom').astype(jnp.float32)]
    dot_general x21 -> x0, matrix products: 49 us -> none  [matmul(): return jnp.dot(left, right, preferred_element_type=jnp.float32)]
    scatter x2 -> x0, local copies, waits for them, and re-layouts: 36.1 us -> none  [local(): jnp.zeros((cell_count, feature_width), jnp.bfloat16).at[mine]]
    reduce_scatter x1 -> x0, waiting for transfers between devices: 27.7 us -> none  [local(): lax.psum_scatter(scaled.astype(jnp.bfloat16), 'dom', scatter_dimension=0,...]
    all_gather x1 -> x0, blocking collectives: 21.4 us -> none  [local(): lax.all_gather(target, 'dom', axis=0, tiled=True)]
    reshape x4 -> x0, local copies, waits for them, and re-layouts: 19.2 us -> none  [the longest x1 5.48 us: layer_math(): jnp.repeat(summed_grad, fan_in, axis=0)]
  transfers between devices with their start and end apart: 8 -> 0, of which waited for: 4 -> 0; matrix products, arithmetic and copies ran while one was open for 17% -> 0% of each run, Pallas kernels for 0% -> 0%
where the time goes in v1:
time: 110 us
  Pallas kernels  105 us (95%)
  local copies, waits for them, and re-layouts  3.68 us (3%)
    pallas_call x1, Pallas kernels, collect(): pl.pallas_call(collect_kernel, out_shape=(jax.ShapeDtypeStruct((C, D), BF...  45.9 us
    pallas_call x1, Pallas kernels, layer(): pl.pallas_call(layer_kernel, grid=(TILES,), out_shape=(jax.ShapeDtypeStru...  31.4 us
    pallas_call x1, Pallas kernels, deliver(): pl.pallas_call(deliver_kernel, out_shape=(jax.ShapeDtypeStruct((PADDED, D...  28 us
    unnamed x2, local copies, waits for them, and re-layouts  3.68 us

profile of v1, /device:TPU:1, one launch (start us, length us, event | category | flops | bytes accessed | tf_op | source)
XLA Modules:
  0.0 109.6 jit_solution(6213500635519206868)
XLA Ops:
  0.6 28.0 %deliver.1 = (bf16[640,512]{1,0:T(8,128)(2,1)}, f32[16,128]{1,0:T(8,128)}, s32[1,512]{1,0:T(1,128)}) custom-call(bf16[512,512]{1,0:T(8,128)(2,1)} %bitcast.13, s32[1,512]{1,0:T(1,128)} %tgt_ref.1), custom_call_target="tpu_custom_call" | custom-call | tf_op jit(solution)/shard_map/deliver/pallas_call | solution.py:145
  28.6 31.4 %layer.1 = (bf16[2048,512]{1,0:T(8,128)(2,1)}, bf16[512,512]{1,0:T(8,128)(2,1)}, bf16[2048,512]{1,0:T(8,128)(2,1)}, f32[512,512]{1,0:T(8,128)}, bf16[2,64,512]{2,1,0:T(8,128)(2,1)}, /*index=5*/bf16[3584,512]{1,0:T(8,128)(2,1)}) custom-call(bf16[640,512]{1,0:T(8,128)(2,1)} %get-tuple-element.16.pad_ref, s32[1,2048]{1,0:T(1,128)} %src_ref.1, ...), custom_call_target="tpu_custom_call" | custom-call | tf_op jit(solution)/shard_map/layer/pallas_call | solution.py:282
  60.0 45.9 %collect.1 = (bf16[512,512]{1,0:T(8,128)(2,1)}, f32[224,512]{1,0:T(8,128)}) custom-call(f32[512,512]{1,0:T(8,128)} %get-tuple-element.19.ng_ref, bf16[2,64,512]{2,1,0:T(8,128)(2,1)} %get-tuple-element.20.halo_ref, bf16[4,4,2,112,512]{4,3,2,1,0:T(8,128)(2,1)} %bitcast.9, f32[16,128]{1,0:T(8,128)} %get-tuple-element.22.ids_ref, ...), custom_call_target="tpu_custom_call" | custom-call | tf_op jit(solution)/shard_map/collect/pallas_call | solution.py:454
  105.9 1.9 %copy.17 = bf16[1,512,512]{2,1,0:T(8,128)(2,1)} copy(bf16[1,512,512]{2,1,0:T(8,128)(2,1)} %bitcast.14) | data formatting | bytes 1048576
  107.8 1.8 %copy.18 = f32[224,512]{1,0:T(8,128)} copy(f32[224,512]{1,0:T(8,128)} %get-tuple-element.36) | data formatting | bytes 917504

commit v2 on v1

--- a/solution.py
+++ b/solution.py
@@ -27,7 +27,6 @@
 RC = 64
 SQUARES = 7
 PER_DOM = SQUARES * D // NP
-PER_CORE = PER_DOM // 2
 
 
 def nn(a, b):
@@ -169,10 +168,9 @@
 
 def layer_kernel(
     pad_ref, src_ref, edges_ref, cotn_ref, cote_ref, wei_ref, weo_ref, wni_ref, wno_ref,
-    edge_new_ref, node_new_ref, grad_edge_ref, ng_ref, halo_ref, w_ref,
-    sel, sel_t, comb, spread, gather4,
-    big, slope, hid, normed, inv, ups, post_grad, pre_grad,
-    total, acc,
+    edge_new_ref, node_new_ref, grad_edge_ref, ng_ref, halo_ref,
+    hid, post_grad, pre_grad, summed_ref, node_hid_ref, node_pre_ref, node_post_ref, recv_ref, send_ref,
+    sel, sel_t, comb, big, slope, normed, inv, ups, total,
 ):
     step = pl.program_id(0)
     me = lax.axis_index("dom")
@@ -186,7 +184,6 @@
         sel[:, PADDED:] = (iota((TE, TC), 0) // K == iota((TE, TC), 1)).astype(BF)
         sel_t[PADDED:, :] = (iota((TC, TE), 1) // K == iota((TC, TE), 0)).astype(BF)
         total[...] = jnp.zeros_like(total)
-        acc[...] = jnp.zeros_like(acc)
 
     nodes = pad_ref[pl.ds(pl.multiple_of(HB + step * TC, HB), TC), :]
     edges = edges_ref[...]
@@ -216,11 +213,13 @@
 
     four = sel_t[PADDED:, :]
     summed = nn(four, edge_new_ref[...]).astype(BF)
+    summed_ref[...] = summed
     v = nn(nodes, w_nself[...]) + nn(summed, w_nagg[...])
     s = sigmoid(v)
     h = v * s
     node_slope = s + h * (1.0 - s)
     node_hid = h.astype(BF)
+    node_hid_ref[...] = node_hid
     v = nn(node_hid, wno_ref[...])
     center = v - jnp.mean(v, axis=-1, keepdims=True)
     i = lax.rsqrt(jnp.mean(center * center, axis=-1, keepdims=True) + 1e-05)
@@ -230,7 +229,9 @@
     m1 = jnp.mean(u, axis=-1, keepdims=True)
     m2 = jnp.mean(u * n, axis=-1, keepdims=True)
     node_post_grad = (i * (u - m1 - n * m2)).astype(BF)
+    node_post_ref[...] = node_post_grad
     node_pre_grad = (nt(node_post_grad, wno_ref[...]) * node_slope).astype(BF)
+    node_pre_ref[...] = node_pre_grad
     spread_grad = nt(node_pre_grad, w_nagg[...]).astype(BF)
 
     ups[...] = nn(sel[:, PADDED:], spread_grad)
@@ -250,26 +251,19 @@
         grad_edge_ref[r : r + RC, :] = (ups[r : r + RC, :] + big[r : r + RC, :]).astype(BF)
     total[...] += nn(sel_t[0:PADDED, :], g)
     recv_grad = nn(four, g).astype(BF)
+    recv_ref[...] = recv_grad
     ng_ref[rows, :] = (
         cotn_ref[...].astype(F32) + nt(node_pre_grad, w_nself[...]) + nt(recv_grad, w_recv[...])
     )
-    acc[0:D, :] += tn(edges, g)
-    acc[2 * D : 3 * D, :] += tn(nodes, recv_grad)
-    acc[3 * D : 4 * D, :] += tn(hid[...], post_grad[...])
-    acc[4 * D : 5 * D, :] += tn(nodes, node_pre_grad)
-    acc[5 * D : 6 * D, :] += tn(summed, node_pre_grad)
-    acc[6 * D : 7 * D, :] += tn(node_hid, node_post_grad)
 
     @pl.when(step == TILES - 1)
     def _():
-        scale = 1.0 / math.sqrt(8 * NP * C * K)
         t = total[...].astype(BF)
-        acc[D : 2 * D, :] = tn(pad_ref[...], t)
+        send_ref[...] = t
         back = nt(t, w_send[...])
         ng_ref[...] += back[HB : HB + C]
         halo_ref[0] = back[0:HB].astype(BF)
         halo_ref[1] = back[HB + C :].astype(BF)
-        w_ref[...] = (acc[...] * scale).astype(BF)
 
 
 def layer(padded, source, edges, cot_nodes, cot_edges, wei, weo, wni, wno):
@@ -279,63 +273,59 @@
     def tile(rows):
         return pl.BlockSpec((rows, D), lambda i: (i, 0))
 
+    by_edge = jax.ShapeDtypeStruct((C * K, D), BF)
+    by_cell = jax.ShapeDtypeStruct((C, D), BF)
     return pl.pallas_call(
         layer_kernel,
         grid=(TILES,),
         out_shape=(
-            jax.ShapeDtypeStruct((C * K, D), BF),
-            jax.ShapeDtypeStruct((C, D), BF),
-            jax.ShapeDtypeStruct((C * K, D), BF),
+            by_edge, by_cell, by_edge,
             jax.ShapeDtypeStruct((C, D), F32),
             jax.ShapeDtypeStruct((2, HB, D), BF),
-            jax.ShapeDtypeStruct((SQUARES * D, D), BF),
+            by_edge, by_edge, by_edge, by_cell, by_cell, by_cell, by_cell, by_cell,
+            jax.ShapeDtypeStruct((PADDED, D), BF),
         ),
         in_specs=[
             whole((PADDED, D)),
             pl.BlockSpec((1, TE), lambda i: (0, i)),
-            tile(TE),
-            tile(TC),
-            tile(TE),
-            whole((3 * D, D)),
-            whole((D, D)),
-            whole((2 * D, D)),
-            whole((D, D)),
+            tile(TE), tile(TC), tile(TE),
+            whole((3 * D, D)), whole((D, D)), whole((2 * D, D)), whole((D, D)),
         ],
         out_specs=(
-            tile(TE),
-            tile(TC),
-            tile(TE),
-            whole((C, D)),
-            whole((2, HB, D)),
-            whole((SQUARES * D, D)),
+            tile(TE), tile(TC), tile(TE),
+            whole((C, D)), whole((2, HB, D)),
+            tile(TE), tile(TE), tile(TE), tile(TC), tile(TC), tile(TC), tile(TC), tile(TC),
+            whole((PADDED, D)),
         ),
         scratch_shapes=[
             pltpu.VMEM((TE, SEL), BF),
             pltpu.VMEM((SEL, TE), BF),
             pltpu.VMEM((SEL, D), BF),
-            pltpu.VMEM((8, 128), BF),
-            pltpu.VMEM((8, 128), BF),
             pltpu.VMEM((TE, D), F32),
             pltpu.VMEM((TE, D), F32),
-            pltpu.VMEM((TE, D), BF),
             pltpu.VMEM((TE, D), F32),
             pltpu.VMEM((TE, 128), F32),
             pltpu.VMEM((TE, D), F32),
-            pltpu.VMEM((TE, D), BF),
-            pltpu.VMEM((TE, D), BF),
             pltpu.VMEM((PADDED, D), F32),
-            pltpu.VMEM((SQUARES * D, D), F32),
         ],
         compiler_params=pltpu.CompilerParams(vmem_limit_bytes=60 * 1024 * 1024),
         name="layer",
     )(padded, source, edges, cot_nodes, cot_edges, wei, weo, wni, wno)
 
 
+ROWS = SQUARES * D
+QW = 128
+CW = 2 * QW
+ORDER = (4, 5, 6, 2, 1, 3, 0)
+
+
 def collect_kernel(
-    ng_ref, halo_ref, w_ref, ids_ref, slot_ref, grad_ref, out_ref,
-    hbuf, sback, rback, pbuf, wsum, r1a, r1b, p1a, p1b, r2a, r2b, r3, fin,
-    hsend, hrecv, bsend, brecv, psend, precv, s1a, v1a, s1b, v1b,
-    s2a, v2a, s2b, v2b, s3, v3, s4, v4,
+    ng_ref, halo_ref, ids_ref,
+    edges_hbm, pad_hbm, hid_hbm, post_hbm, pre_hbm, summed_hbm, nhid_hbm, npre_hbm, npost_hbm, recv_hbm, send_hbm,
+    back_ref, fin_ref,
+    edges, pad, hid, post, pre, summed, nhid, npre, npost, recv_g, send_g,
+    hbuf, sback, rback, wown, wsend, pbuf, wsum, r1, p1, r2, r3, fin,
+    lsem, hsend, hrecv, bsend, brecv, psend, precv, s1, v1, s2, v2, s3, v3, s4, v4,
 ):
     geom = lax.axis_index("geom")
     me = lax.axis_index("dom")
@@ -344,32 +334,74 @@
     y = me // 4
     z = me % 4
     partner = x * 2 + (1 - core)
+    i_me = y * (1 - core) + z * core
+    j_me = z * (1 - core) + y * core
+
+    def dom_of(i, j):
+        return (i * 4 + j) * (1 - core) + (j * 4 + i) * core
+
     barrier = pltpu.get_barrier_semaphore()
-    signal(barrier, partner, me)
+    signals = NP - 1
     for p in range(1, NP):
         signal(barrier, geom, (me + p) % NP)
+    signal(barrier, partner, me)
     for d in range(1, 4):
         signal(barrier, ((x + d) % 4) * 2 + core, me)
-    pl.semaphore_wait(barrier, NP + 3)
-
+    signals += 4
+
+    pairs = (
+        (npre_hbm, npre), (pad_hbm, pad), (summed_hbm, summed), (npost_hbm, npost), (nhid_hbm, nhid),
+        (recv_hbm, recv_g), (send_hbm, send_g), (post_hbm, post), (hid_hbm, hid), (pre_hbm, pre), (edges_hbm, edges),
+    )
+    loads = {}
+    for n, (far, near) in enumerate(pairs):
+        loads[id(near)] = pltpu.make_async_copy(far, near, lsem.at[n])
+        loads[id(near)].start()
+
+    def ready(*refs):
+        for ref in refs:
+            if id(ref) in loads:
+                loads.pop(id(ref)).wait()
+
+    scale = 1.0 / math.sqrt(8 * NP * C * K)
+    inner = slice(HB, HB + C)
+    operands = {
+        0: (edges, None, pre), 1: (pad, None, send_g), 2: (pad, inner, recv_g), 3: (hid, None, post),
+        4: (pad, inner, npre), 5: (summed, None, npre), 6: (nhid, None, npost),
+    }
+    pair = {}
+
+    def square(c, q):
+        left, cut, right = operands[q]
+        ready(left, right)
+        rows = left[...] if cut is None else left[cut, :]
+        value = (tn(rows, right[:, c * CW : (c + 1) * CW]) * scale).astype(BF)
+        low, high = value[:, 0:QW], value[:, QW:CW]
+        wown[c, q] = jnp.where(core == 0, low, high)
+        wsend[c, q] = jnp.where(core == 0, high, low)
+        n = c * SQUARES + q
+        pair[c, q] = remote(wsend.at[c, q], pbuf.at[c, q], psend.at[n], precv.at[n], partner, me)
+
+    for q in ORDER[:3]:
+        square(0, q)
+    pl.semaphore_wait(barrier, signals)
     to_prev = remote(halo_ref.at[0], hbuf.at[1], hsend.at[0], hrecv.at[1], geom, (me + NP - 1) % NP)
     to_next = remote(halo_ref.at[1], hbuf.at[0], hsend.at[1], hrecv.at[0], geom, (me + 1) % NP)
     to_prev.start()
     to_next.start()
-    pair = [
-        remote(w_ref.at[i, :, 1 - core], pbuf.at[i], psend.at[i], precv.at[i], partner, me)
-        for i in range(4)
-    ]
-    for copy in pair:
-        copy.start()
-
-    blocks = unpack_blocks(ids_ref[...])
+    for q in ORDER[:3]:
+        pair[0, q].start()
+    for q in ORDER[3:5]:
+        square(0, q)
+        pair[0, q].start()
+
+    blocks = jnp.concatenate(unpack_blocks(ids_ref[...]), axis=0)
     to_prev.wait_recv()
     to_next.wait_recv()
     first = ng_ref[0:HB, :] + hbuf[0].astype(F32)
     last = ng_ref[C - HB :, :] + hbuf[1].astype(F32)
     cells = jnp.concatenate([first, ng_ref[HB : C - HB, :], last], axis=0).astype(BF)
-    packed = nn(jnp.concatenate(blocks, axis=0), cells).astype(BF)
+    packed = nn(blocks, cells).astype(BF)
     sback[...] = packed.reshape(NP, CAP, D)
     rback[0] = packed[0:CAP]
     backs = [
@@ -379,118 +411,163 @@
     for copy in backs:
         copy.start()
 
-    for i in range(4):
-        pair[i].wait_recv()
+    for q in ORDER[5:]:
+        square(0, q)
+        pair[0, q].start()
+
+    ones = {}
+
+    def join(c):
+        for q in ORDER:
+            pair[c, q].wait_recv()
+        for k in range(NP):
+            parts = []
+            at, end = k * PER_DOM, (k + 1) * PER_DOM
+            while at < end:
+                q, r = divmod(at, D)
+                n = min(end - at, D - r)
+                parts.append(wown[c, q, r : r + n].astype(F32) + pbuf[c, q, r : r + n].astype(F32))
+                at += n
+            value = parts[0] if len(parts) == 1 else jnp.concatenate(parts, axis=0)
+            i = (k // 4) * (1 - core) + (k % 4) * core
+            j = (k % 4) * (1 - core) + (k // 4) * core
+            wsum[c, pl.ds(i * 4 + j, 1)] = value.astype(BF).reshape(1, PER_DOM, QW)
+        for d in range(1, 4):
+            n = c * 3 + d - 1
+            ones[c, d] = remote(
+                wsum.at[c, pl.ds(((i_me + d) % 4) * 4, 4)], r1.at[c, d - 1], s1.at[n], v1.at[n],
+                geom, dom_of((i_me + d) % 4, j_me),
+            )
+            ones[c, d].start()
+
+    twos, threes, fours = {}, {}, {}
+
+    def narrow(c):
+        for d in range(1, 4):
+            ones[c, d].wait_recv()
         for j in range(4):
-            mine = w_ref[i, j, pl.ds(core, 1)].reshape(PER_CORE, D)
-            wsum[i, j] = (mine.astype(F32) + pbuf[i, j].astype(F32)).astype(BF)
-
-    half = D // 2
-    ones = []
-    for d in range(1, 4):
-        ty, tz = (y + d) % 4, (z + d) % 4
-        ones.append(
-            remote(wsum.at[ty, :, :, 0:half], r1a.at[d - 1], s1a.at[d - 1], v1a.at[d - 1], geom, ty * 4 + z)
-        )
-        ones.append(
-            remote(wsum.at[:, tz, :, half:D], r1b.at[d - 1], s1b.at[d - 1], v1b.at[d - 1], geom, y * 4 + tz)
-        )
-    for copy in ones:
-        copy.start()
-
+            own = wsum[c, pl.ds(i_me * 4 + j, 1)].reshape(PER_DOM, QW).astype(F32)
+            for d in range(3):
+                own += r1[c, d, j].astype(F32)
+            p1[c, j] = own.astype(BF)
+        for d in range(1, 4):
+            n = c * 3 + d - 1
+            j = (j_me + d) % 4
+            twos[c, d] = remote(p1.at[c, j], r2.at[c, d - 1], s2.at[n], v2.at[n], geom, dom_of(i_me, j))
+            twos[c, d].start()
+
+    def across(c):
+        for d in range(1, 4):
+            twos[c, d].wait_recv()
+        own = p1[c, pl.ds(j_me, 1)].reshape(PER_DOM, QW).astype(F32)
+        for d in range(3):
+            own += r2[c, d].astype(F32)
+        r3[c, pl.ds(x, 1)] = own.astype(BF).reshape(1, PER_DOM, QW)
+        for d in range(1, 4):
+            n = c * 3 + d - 1
+            threes[c, d] = remote(
+                r3.at[c, x], r3.at[c, x], s3.at[n], v3.at[n], ((x + d) % 4) * 2 + core, me
+            )
+            threes[c, d].start()
+
+    def last_sum(c):
+        for d in range(1, 4):
+            n = c * 3 + d - 1
+            origin = (x + 4 - d) % 4
+            remote(r3.at[c, x], r3.at[c, origin], s3.at[n], v3.at[n], origin * 2 + core, me).wait_recv()
+        done = r3[c, 0].astype(F32) + r3[c, 1].astype(F32) + r3[c, 2].astype(F32) + r3[c, 3].astype(F32)
+        fin[c, pl.ds(core, 1)] = done.astype(BF).reshape(1, PER_DOM, QW)
+        fours[c] = remote(fin.at[c, core], fin.at[c, core], s4.at[c], v4.at[c], partner, me)
+        fours[c].start()
+
+    join(0)
+    for q in ORDER:
+        square(1, q)
+        pair[1, q].start()
+    join(1)
+    narrow(0)
+    narrow(1)
+    across(0)
+    across(1)
     for copy in backs:
         copy.wait_recv()
-    grad_ref[...] = tn(pack_matrix(slot_ref[...]), rback[...].reshape(SLOTS, D)).astype(BF)
-
-    for copy in ones:
-        copy.wait_recv()
-    for j in range(4):
-        own = wsum[pl.ds(y, 1), j, :, 0:half].reshape(PER_CORE, half).astype(F32)
-        for d in range(3):
-            own += r1a[d, j].astype(F32)
-        p1a[j] = own.astype(BF)
-        own = wsum[j, pl.ds(z, 1), :, half:D].reshape(PER_CORE, half).astype(F32)
-        for d in range(3):
-            own += r1b[d, j].astype(F32)
-        p1b[j] = own.astype(BF)
-    twos = []
-    for d in range(1, 4):
-        ty, tz = (y + d) % 4, (z + d) % 4
-        twos.append(remote(p1a.at[tz], r2a.at[d - 1], s2a.at[d - 1], v2a.at[d - 1], geom, y * 4 + tz))
-        twos.append(remote(p1b.at[ty], r2b.at[d - 1], s2b.at[d - 1], v2b.at[d - 1], geom, ty * 4 + z))
-    for copy in twos:
-        copy.start()
-    for copy in twos:
-        copy.wait_recv()
-    left = p1a[pl.ds(z, 1)].reshape(PER_CORE, half).astype(F32)
-    right = p1b[pl.ds(y, 1)].reshape(PER_CORE, half).astype(F32)
-    for d in range(3):
-        left += r2a[d].astype(F32)
-        right += r2b[d].astype(F32)
-    r3[pl.ds(x, 1)] = jnp.concatenate([left, right], axis=1).astype(BF).reshape(1, PER_CORE, D)
-    threes = [
-        remote(r3.at[x], r3.at[x], s3.at[d - 1], v3.at[d - 1], ((x + d) % 4) * 2 + core, me)
-        for d in range(1, 4)
-    ]
-    for copy in threes:
-        copy.start()
-    for d in range(1, 4):
-        source = (x + 4 - d) % 4
-        remote(r3.at[x], r3.at[source], s3.at[d - 1], v3.at[d - 1], source * 2 + core, me).wait_recv()
-    done = r3[0].astype(F32) + r3[1].astype(F32) + r3[2].astype(F32) + r3[3].astype(F32)
-    fin[pl.ds(core, 1)] = done.reshape(1, PER_CORE, D)
-    four = remote(fin.at[core], fin.at[core], s4, v4, partner, me)
-    four.start()
-    remote(fin.at[core], fin.at[1 - core], s4, v4, partner, me).wait_recv()
-    out_ref[...] = fin[...].reshape(PER_DOM, D)
-    for copy in [to_prev, to_next] + pair + backs + ones + twos + threes + [four]:
+    last_sum(0)
+    last_sum(1)
+    for c in range(2):
+        remote(fin.at[c, core], fin.at[c, 1 - core], s4.at[c], v4.at[c], partner, me).wait_recv()
+    back_ref[...] = rback[...].reshape(SLOTS, D)
+    for c in range(2):
+        for q in range(2):
+            fin_ref[:, c * CW + q * QW : c * CW + (q + 1) * QW] = fin[c, q]
+    groups = (pair, ones, twos, threes, fours)
+    for copy in [to_prev, to_next] + backs + [copy for group in groups for copy in group.values()]:
         copy.wait_send()
 
 
-def collect(ng, halo, w, ids, slot):
+def finish_kernel(back_ref, slot_ref, fin_ref, grad_ref, out_ref):
+    grad_ref[...] = tn(pack_matrix(slot_ref[...]), back_ref[...]).astype(BF)
+    out_ref[...] = fin_ref[...].astype(F32)
+
+
+def finish(back, slot, fin):
     vm = pl.BlockSpec(memory_space=pltpu.VMEM)
-    half = D // 2
+    return pl.pallas_call(
+        finish_kernel,
+        out_shape=(jax.ShapeDtypeStruct((C, D), BF), jax.ShapeDtypeStruct((PER_DOM, D), F32)),
+        in_specs=[vm] * 3,
+        out_specs=(vm, vm),
+        name="finish",
+    )(back, slot, fin)
+
+
+def collect(ng, halo, ids, *operands):
+    vm = pl.BlockSpec(memory_space=pltpu.VMEM)
+    hbm = pl.BlockSpec(memory_space=pl.ANY)
     dma = pltpu.SemaphoreType.DMA
     return pl.pallas_call(
         collect_kernel,
         out_shape=(
-            jax.ShapeDtypeStruct((C, D), BF),
-            jax.ShapeDtypeStruct((PER_DOM, D), F32),
-        ),
-        in_specs=[vm] * 5,
+            jax.ShapeDtypeStruct((SLOTS, D), BF),
+            jax.ShapeDtypeStruct((PER_DOM, D), BF),
+        ),
+        in_specs=[vm] * 3 + [hbm] * len(operands),
         out_specs=(vm, vm),
-        scratch_shapes=[
+        scratch_shapes=[pltpu.VMEM(a.shape, a.dtype) for a in operands]
+        + [
             pltpu.VMEM((2, HB, D), BF),
             pltpu.VMEM((NP, CAP, D), BF),
             pltpu.VMEM((NP, CAP, D), BF),
-            pltpu.VMEM((4, 4, PER_CORE, D), BF),
-            pltpu.VMEM((4, 4, PER_CORE, D), BF),
-            pltpu.VMEM((3, 4, PER_CORE, half), BF),
-            pltpu.VMEM((3, 4, PER_CORE, half), BF),
-            pltpu.VMEM((4, PER_CORE, half), BF),
-            pltpu.VMEM((4, PER_CORE, half), BF),
-            pltpu.VMEM((3, PER_CORE, half), BF),
-            pltpu.VMEM((3, PER_CORE, half), BF),
-            pltpu.VMEM((4, PER_CORE, D), BF),
-            pltpu.VMEM((2, PER_CORE, D), F32),
-            dma((2,)), dma((2,)), dma((NP,)), dma((NP,)), dma((4,)), dma((4,)),
-            dma((3,)), dma((3,)), dma((3,)), dma((3,)),
-            dma((3,)), dma((3,)), dma((3,)), dma((3,)),
-            dma((3,)), dma((3,)), dma, dma,
+            pltpu.VMEM((2, SQUARES, D, QW), BF),
+            pltpu.VMEM((2, SQUARES, D, QW), BF),
+            pltpu.VMEM((2, SQUARES, D, QW), BF),
+            pltpu.VMEM((2, NP, PER_DOM, QW), BF),
+            pltpu.VMEM((2, 3, 4, PER_DOM, QW), BF),
+            pltpu.VMEM((2, 4, PER_DOM, QW), BF),
+            pltpu.VMEM((2, 3, PER_DOM, QW), BF),
+            pltpu.VMEM((2, 4, PER_DOM, QW), BF),
+            pltpu.VMEM((2, 2, PER_DOM, QW), BF),
+            dma((len(operands),)), dma((2,)), dma((2,)), dma((NP,)), dma((NP,)),
+            dma((2 * SQUARES,)), dma((2 * SQUARES,)), dma((6,)), dma((6,)),
+            dma((6,)), dma((6,)), dma((6,)), dma((6,)), dma((2,)), dma((2,)),
         ],
-        compiler_params=pltpu.CompilerParams(collective_id=1, has_side_effects=True),
+        compiler_params=pltpu.CompilerParams(
+            collective_id=1, has_side_effects=True, vmem_limit_bytes=60 * 1024 * 1024
+        ),
         name="collect",
-    )(ng, halo, w, ids, slot)
+    )(ng, halo, ids, *operands)
 
 
 def local(
     h_in, edge_in, new_index, source, w_edge_in, w_edge_out, w_node_in, w_node_out, cot_nodes, cot_edges
 ):
     padded, ids, slot = deliver(h_in[0], new_index)
-    edge_new, node_new, grad_edge, ng, halo, w = layer(
+    edge_new, node_new, grad_edge, ng, halo, hid, post, pre, summed, nhid, npre, npost, recv, send = layer(
         padded, source, edge_in[0], cot_nodes[0], cot_edges[0], w_edge_in, w_edge_out, w_node_in, w_node_out
     )
-    grad_in, weight_grads = collect(ng, halo, w.reshape(4, 4, 2, PER_CORE, D), ids, slot)
+    back, fin = collect(
+        ng, halo, ids, edge_in[0], padded, hid, post, pre, summed, nhid, npre, npost, recv, send
+    )
+    grad_in, weight_grads = finish(back, slot, fin)
     return (node_new[None], edge_new[None], grad_in[None], grad_edge[None], weight_grads)
 
 

time: 110 us -> 102 us (0.927)
  Pallas kernels: 105 us -> 101 us
  local copies, waits for them, and re-layouts: 3.68 us -> 0 us
    pallas_call x2 -> x3, Pallas kernels: 77.3 us -> 73.1 us  [the longest x1 44.5 us: collect(): pl.pallas_call(collect_kernel, out_shape=(jax.ShapeDtypeStruct((SLOTS, D)...]
    unnamed x2 -> x0, local copies, waits for them, and re-layouts: 3.68 us -> none
where the time goes in v2:
time: 102 us
  Pallas kernels  101 us (99%)
    pallas_call x1, Pallas kernels, collect(): pl.pallas_call(collect_kernel, out_shape=(jax.ShapeDtypeStruct((SLOTS, D)...  44.5 us
    pallas_call x1, Pallas kernels, deliver(): pl.pallas_call(deliver_kernel, out_shape=(jax.ShapeDtypeStruct((PADDED, D...  28 us
    pallas_call x1, Pallas kernels, layer(): pl.pallas_call(layer_kernel, grid=(TILES,), out_shape=(by_edge, by_cell,...  26 us
    pallas_call x1, Pallas kernels, finish(): pl.pallas_call(finish_kernel, out_shape=(jax.ShapeDtypeStruct((C, D), BF)...  2.69 us

profile of v2, /device:TPU:1, one launch (start us, length us, event | category | flops | bytes accessed | tf_op | source)
XLA Modules:
  0.0 101.8 jit_solution(4802161692951778146)
XLA Ops:
  0.6 28.0 %deliver.1 = (bf16[640,512]{1,0:T(8,128)(2,1)}, f32[16,128]{1,0:T(8,128)}, s32[1,512]{1,0:T(1,128)}) custom-call(bf16[512,512]{1,0:T(8,128)(2,1)} %bitcast.12, s32[1,512]{1,0:T(1,128)} %tgt_ref.1), custom_call_target="tpu_custom_call" | custom-call | tf_op jit(solution)/shard_map/deliver/pallas_call | solution.py:144
  28.7 26.0 %layer.1 = (bf16[2048,512]{1,0:T(8,128)(2,1)}, bf16[512,512]{1,0:T(8,128)(2,1)}, bf16[2048,512]{1,0:T(8,128)(2,1)}, f32[512,512]{1,0:T(8,128)}, bf16[2,64,512]{2...) custom-call(bf16[640,512]{1,0:T(8,128)(2,1)} %get-tuple-element.26.p, ...), custom_call_target="tpu_custom_call" | custom-call | tf_op jit(solution)/shard_map/layer/pallas_call | solution.py:278
  54.6 44.5 %collect.1 = (bf16[768,512]{1,0:T(8,128)(2,1)}, bf16[224,512]{1,0:T(8,128)(2,1)}) custom-call(f32[512,512]{1,0:T(8,128)} %get-tuple-element.29.ng_ref, bf16[2,64,512]{2,1,0:T(8,128)(2,1)} %get-tuple-element.30.halo_ref, f32[16,128]{1,0:T(8,128)} %get-tuple-element.31.ids_ref, bf16[2048,512]{1,0:T(8,128)(2,1)} %bitcast.9, ...), custom_call_target="tpu_custom_call" | custom-call | tf_op jit(solution)/shard_map/collect/pallas_call | solution.py:527
  99.1 2.7 %finish.1 = (bf16[512,512]{1,0:T(8,128)(2,1)}, f32[224,512]{1,0:T(8,128)}) custom-call(bf16[768,512]{1,0:T(8,128)(2,1)} %get-tuple-element.41.back_ref, s32[1,512]{1,0:T(1,128)} %get-tuple-element.42.slot_ref, bf16[224,512]{1,0:T(8,128)(2,1)} %get-tuple-element.43.fin_ref), custom_call_target="tpu_custom_call" | custom-call | tf_op jit(solution)/shard_map/finish/pallas_call | solution.py:514

commit v3 on v2

--- a/solution.py
+++ b/solution.py
@@ -316,7 +316,9 @@
 ROWS = SQUARES * D
 QW = 128
 CW = 2 * QW
-ORDER = (4, 5, 6, 2, 1, 3, 0)
+EARLY = 10
+PART = 64
+STARTS = (0, 64, 128, 160)
 
 
 def collect_kernel(
@@ -324,8 +326,8 @@
     edges_hbm, pad_hbm, hid_hbm, post_hbm, pre_hbm, summed_hbm, nhid_hbm, npre_hbm, npost_hbm, recv_hbm, send_hbm,
     back_ref, fin_ref,
     edges, pad, hid, post, pre, summed, nhid, npre, npost, recv_g, send_g,
-    hbuf, sback, rback, wown, wsend, pbuf, wsum, r1, p1, r2, r3, fin,
-    lsem, hsend, hrecv, bsend, brecv, psend, precv, s1, v1, s2, v2, s3, v3, s4, v4,
+    hbuf, sback, rback, wown, wsend, pbuf, wsum, r1, p1, r2, r3, fin, wx, rx, px, ri, ag,
+    lsem, hsend, hrecv, bsend, brecv, psend, precv, s1, v1, s2, v2, s3, v3, s4, v4, sx, vx, si, vi, sg, vg,
 ):
     geom = lax.axis_index("geom")
     me = lax.axis_index("dom")
@@ -344,14 +346,13 @@
     signals = NP - 1
     for p in range(1, NP):
         signal(barrier, geom, (me + p) % NP)
-    signal(barrier, partner, me)
-    for d in range(1, 4):
-        signal(barrier, ((x + d) % 4) * 2 + core, me)
-    signals += 4
+    for d in range(1, 8):
+        signal(barrier, (geom + d) % 8, me)
+        signals += 1
 
     pairs = (
         (npre_hbm, npre), (pad_hbm, pad), (summed_hbm, summed), (npost_hbm, npost), (nhid_hbm, nhid),
-        (recv_hbm, recv_g), (send_hbm, send_g), (post_hbm, post), (hid_hbm, hid), (pre_hbm, pre), (edges_hbm, edges),
+        (post_hbm, post), (hid_hbm, hid), (recv_hbm, recv_g), (send_hbm, send_g), (pre_hbm, pre), (edges_hbm, edges),
     )
     loads = {}
     for n, (far, near) in enumerate(pairs):
@@ -371,29 +372,142 @@
     }
     pair = {}
 
-    def square(c, q):
+    def square(q):
         left, cut, right = operands[q]
         ready(left, right)
         rows = left[...] if cut is None else left[cut, :]
-        value = (tn(rows, right[:, c * CW : (c + 1) * CW]) * scale).astype(BF)
-        low, high = value[:, 0:QW], value[:, QW:CW]
-        wown[c, q] = jnp.where(core == 0, low, high)
-        wsend[c, q] = jnp.where(core == 0, high, low)
-        n = c * SQUARES + q
-        pair[c, q] = remote(wsend.at[c, q], pbuf.at[c, q], psend.at[n], precv.at[n], partner, me)
-
-    for q in ORDER[:3]:
-        square(0, q)
+        value = (tn(rows, right[...]) * scale).astype(BF)
+        for c in range(2):
+            low, high = value[:, c * CW : c * CW + QW], value[:, c * CW + QW : (c + 1) * CW]
+            wown[c, q] = jnp.where(core == 0, low, high)
+            wsend[c, q] = jnp.where(core == 0, high, low)
+            n = c * SQUARES + q
+            pair[c, q] = remote(wsend.at[c, q], pbuf.at[c, q], psend.at[n], precv.at[n], partner, me)
+
+    def reduced_block(c, k):
+        parts = []
+        at, end = k * PER_DOM, (k + 1) * PER_DOM
+        while at < end:
+            q, r = divmod(at, D)
+            n = min(end - at, D - r)
+            parts.append(wown[c, q, r : r + n].astype(F32) + pbuf[c, q, r : r + n].astype(F32))
+            at += n
+        value = parts[0] if len(parts) == 1 else jnp.concatenate(parts, axis=0)
+        return value.astype(BF)
+
+    seen = set()
+
+    def joined(c, squares):
+        for q in squares:
+            if (c, q) not in seen:
+                seen.add((c, q))
+                pair[c, q].wait_recv()
+
+    ones, xs, ys = {}, [], []
+
+    def join(c):
+        joined(c, range(SQUARES))
+        for k in range(NP):
+            i = (k // 4) * (1 - core) + (k % 4) * core
+            j = (k % 4) * (1 - core) + (k // 4) * core
+            wsum[pl.ds(i * 4 + j, 1)] = reduced_block(c, k).reshape(1, PER_DOM, QW)
+        for d in range(1, 4):
+            to = (i_me + d) % 4
+            ones[d] = remote(
+                wsum.at[pl.ds(to * 4, 4)], r1.at[d - 1], s1.at[d - 1], v1.at[d - 1], geom, dom_of(to, j_me)
+            )
+            ones[d].start()
+
+    def join_x(c, low, high, squares):
+        joined(c, squares)
+        for k in range(low, high):
+            value = reduced_block(c, k)
+            for n, r in enumerate(STARTS):
+                wx[n, k] = value[r : r + PART]
+        for d in range(1, 4):
+            to = (x + d) % 4
+            n = len(xs)
+            xs.append(
+                remote(
+                    wx.at[to, low:high], rx.at[d - 1, low:high], sx.at[n], vx.at[n], to * 2 + core, me
+                )
+            )
+            xs[-1].start()
+
+    def narrow_x():
+        for copy in xs:
+            copy.wait_recv()
+        own = wx[pl.ds(x, 1)].reshape(NP, PART, QW).astype(F32)
+        for d in range(3):
+            own += rx[d].astype(F32)
+        px[...] = own.astype(BF)
+        for d in range(1, NP):
+            to = (me + d) % NP
+            ys.append(remote(px.at[to], ri.at[d - 1], si.at[d - 1], vi.at[d - 1], geom, to))
+            ys[-1].start()
+
+    gathers = []
+
+    def narrow_dom():
+        for copy in ys:
+            copy.wait_recv()
+        own = px[pl.ds(me, 1)].reshape(PART, QW).astype(F32)
+        for d in range(NP - 1):
+            own += ri[d].astype(F32)
+        ag[pl.ds(geom, 1)] = own.astype(BF).reshape(1, PART, QW)
+        for d in range(1, 8):
+            gathers.append(
+                remote(ag.at[geom], ag.at[geom], sg.at[d - 1], vg.at[d - 1], (geom + d) % 8, me)
+            )
+            gathers[-1].start()
+
+    twos, threes = {}, {}
+
+    def narrow():
+        for d in range(1, 4):
+            ones[d].wait_recv()
+        for j in range(4):
+            own = wsum[pl.ds(i_me * 4 + j, 1)].reshape(PER_DOM, QW).astype(F32)
+            for d in range(3):
+                own += r1[d, j].astype(F32)
+            p1[j] = own.astype(BF)
+        for d in range(1, 4):
+            j = (j_me + d) % 4
+            twos[d] = remote(p1.at[j], r2.at[d - 1], s2.at[d - 1], v2.at[d - 1], geom, dom_of(i_me, j))
+            twos[d].start()
+
+    def across():
+        for d in range(1, 4):
+            twos[d].wait_recv()
+        own = p1[pl.ds(j_me, 1)].reshape(PER_DOM, QW).astype(F32)
+        for d in range(3):
+            own += r2[d].astype(F32)
+        r3[pl.ds(x, 1)] = own.astype(BF).reshape(1, PER_DOM, QW)
+        for d in range(1, 4):
+            threes[d] = remote(r3.at[x], r3.at[x], s3.at[d - 1], v3.at[d - 1], ((x + d) % 4) * 2 + core, me)
+            threes[d].start()
+
+    def send_pairs(*squares):
+        for c in (1, 0):
+            for q in squares:
+                pair[c, q].start()
+
+    for q in (4, 5, 6):
+        square(q)
     pl.semaphore_wait(barrier, signals)
+    send_pairs(4, 5, 6)
     to_prev = remote(halo_ref.at[0], hbuf.at[1], hsend.at[0], hrecv.at[1], geom, (me + NP - 1) % NP)
     to_next = remote(halo_ref.at[1], hbuf.at[0], hsend.at[1], hrecv.at[0], geom, (me + 1) % NP)
     to_prev.start()
     to_next.start()
-    for q in ORDER[:3]:
-        pair[0, q].start()
-    for q in ORDER[3:5]:
-        square(0, q)
-        pair[0, q].start()
+    square(3)
+    send_pairs(3)
+    join_x(1, EARLY, NP, (4, 5, 6))
+    for q in (2, 1, 0):
+        square(q)
+        send_pairs(q)
+    join_x(1, 0, EARLY, range(SQUARES))
+    join(0)
 
     blocks = jnp.concatenate(unpack_blocks(ids_ref[...]), axis=0)
     to_prev.wait_recv()
@@ -411,97 +525,35 @@
     for copy in backs:
         copy.start()
 
-    for q in ORDER[5:]:
-        square(0, q)
-        pair[0, q].start()
-
-    ones = {}
-
-    def join(c):
-        for q in ORDER:
-            pair[c, q].wait_recv()
-        for k in range(NP):
-            parts = []
-            at, end = k * PER_DOM, (k + 1) * PER_DOM
-            while at < end:
-                q, r = divmod(at, D)
-                n = min(end - at, D - r)
-                parts.append(wown[c, q, r : r + n].astype(F32) + pbuf[c, q, r : r + n].astype(F32))
-                at += n
-            value = parts[0] if len(parts) == 1 else jnp.concatenate(parts, axis=0)
-            i = (k // 4) * (1 - core) + (k % 4) * core
-            j = (k % 4) * (1 - core) + (k // 4) * core
-            wsum[c, pl.ds(i * 4 + j, 1)] = value.astype(BF).reshape(1, PER_DOM, QW)
-        for d in range(1, 4):
-            n = c * 3 + d - 1
-            ones[c, d] = remote(
-                wsum.at[c, pl.ds(((i_me + d) % 4) * 4, 4)], r1.at[c, d - 1], s1.at[n], v1.at[n],
-                geom, dom_of((i_me + d) % 4, j_me),
-            )
-            ones[c, d].start()
-
-    twos, threes, fours = {}, {}, {}
-
-    def narrow(c):
-        for d in range(1, 4):
-            ones[c, d].wait_recv()
-        for j in range(4):
-            own = wsum[c, pl.ds(i_me * 4 + j, 1)].reshape(PER_DOM, QW).astype(F32)
-            for d in range(3):
-                own += r1[c, d, j].astype(F32)
-            p1[c, j] = own.astype(BF)
-        for d in range(1, 4):
-            n = c * 3 + d - 1
-            j = (j_me + d) % 4
-            twos[c, d] = remote(p1.at[c, j], r2.at[c, d - 1], s2.at[n], v2.at[n], geom, dom_of(i_me, j))
-            twos[c, d].start()
-
-    def across(c):
-        for d in range(1, 4):
-            twos[c, d].wait_recv()
-        own = p1[c, pl.ds(j_me, 1)].reshape(PER_DOM, QW).astype(F32)
-        for d in range(3):
-            own += r2[c, d].astype(F32)
-        r3[c, pl.ds(x, 1)] = own.astype(BF).reshape(1, PER_DOM, QW)
-        for d in range(1, 4):
-            n = c * 3 + d - 1
-            threes[c, d] = remote(
-                r3.at[c, x], r3.at[c, x], s3.at[n], v3.at[n], ((x + d) % 4) * 2 + core, me
-            )
-            threes[c, d].start()
-
-    def last_sum(c):
-        for d in range(1, 4):
-            n = c * 3 + d - 1
-            origin = (x + 4 - d) % 4
-            remote(r3.at[c, x], r3.at[c, origin], s3.at[n], v3.at[n], origin * 2 + core, me).wait_recv()
-        done = r3[c, 0].astype(F32) + r3[c, 1].astype(F32) + r3[c, 2].astype(F32) + r3[c, 3].astype(F32)
-        fin[c, pl.ds(core, 1)] = done.astype(BF).reshape(1, PER_DOM, QW)
-        fours[c] = remote(fin.at[c, core], fin.at[c, core], s4.at[c], v4.at[c], partner, me)
-        fours[c].start()
-
-    join(0)
-    for q in ORDER:
-        square(1, q)
-        pair[1, q].start()
-    join(1)
-    narrow(0)
-    narrow(1)
-    across(0)
-    across(1)
+    narrow_x()
+    narrow()
+    across()
+    narrow_dom()
     for copy in backs:
         copy.wait_recv()
-    last_sum(0)
-    last_sum(1)
-    for c in range(2):
-        remote(fin.at[c, core], fin.at[c, 1 - core], s4.at[c], v4.at[c], partner, me).wait_recv()
     back_ref[...] = rback[...].reshape(SLOTS, D)
-    for c in range(2):
-        for q in range(2):
-            fin_ref[:, c * CW + q * QW : c * CW + (q + 1) * QW] = fin[c, q]
-    groups = (pair, ones, twos, threes, fours)
-    for copy in [to_prev, to_next] + backs + [copy for group in groups for copy in group.values()]:
+    for d in range(1, 4):
+        origin = (x + 4 - d) % 4
+        remote(r3.at[x], r3.at[origin], s3.at[d - 1], v3.at[d - 1], origin * 2 + core, me).wait_recv()
+    done = r3[0].astype(F32) + r3[1].astype(F32) + r3[2].astype(F32) + r3[3].astype(F32)
+    fin[pl.ds(core, 1)] = done.astype(BF).reshape(1, PER_DOM, QW)
+    four = remote(fin.at[core], fin.at[core], s4, v4, partner, me)
+    four.start()
+    for d in range(1, 8):
+        origin = (geom + 8 - d) % 8
+        remote(ag.at[geom], ag.at[origin], sg.at[d - 1], vg.at[d - 1], origin, me).wait_recv()
+    for q in range(2):
+        for n, r in enumerate(STARTS):
+            fin_ref[r : r + PART, CW + q * QW : CW + (q + 1) * QW] = ag[n * 2 + q]
+    remote(fin.at[core], fin.at[1 - core], s4, v4, partner, me).wait_recv()
+    for q in range(2):
+        fin_ref[:, q * QW : (q + 1) * QW] = fin[q]
+    groups = (pair, ones, twos, threes)
+    for copy in [to_prev, to_next, four] + backs + xs + ys + gathers:
         copy.wait_send()
+    for group in groups:
+        for copy in group.values():
+            copy.wait_send()
 
 
 def finish_kernel(back_ref, slot_ref, fin_ref, grad_ref, out_ref):
@@ -540,15 +592,21 @@
             pltpu.VMEM((2, SQUARES, D, QW), BF),
             pltpu.VMEM((2, SQUARES, D, QW), BF),
             pltpu.VMEM((2, SQUARES, D, QW), BF),
-            pltpu.VMEM((2, NP, PER_DOM, QW), BF),
-            pltpu.VMEM((2, 3, 4, PER_DOM, QW), BF),
-            pltpu.VMEM((2, 4, PER_DOM, QW), BF),
-            pltpu.VMEM((2, 3, PER_DOM, QW), BF),
-            pltpu.VMEM((2, 4, PER_DOM, QW), BF),
-            pltpu.VMEM((2, 2, PER_DOM, QW), BF),
+            pltpu.VMEM((NP, PER_DOM, QW), BF),
+            pltpu.VMEM((3, 4, PER_DOM, QW), BF),
+            pltpu.VMEM((4, PER_DOM, QW), BF),
+            pltpu.VMEM((3, PER_DOM, QW), BF),
+            pltpu.VMEM((4, PER_DOM, QW), BF),
+            pltpu.VMEM((2, PER_DOM, QW), BF),
+            pltpu.VMEM((4, NP, PART, QW), BF),
+            pltpu.VMEM((3, NP, PART, QW), BF),
+            pltpu.VMEM((NP, PART, QW), BF),
+            pltpu.VMEM((NP - 1, PART, QW), BF),
+            pltpu.VMEM((8, PART, QW), BF),
             dma((len(operands),)), dma((2,)), dma((2,)), dma((NP,)), dma((NP,)),
-            dma((2 * SQUARES,)), dma((2 * SQUARES,)), dma((6,)), dma((6,)),
-            dma((6,)), dma((6,)), dma((6,)), dma((6,)), dma((2,)), dma((2,)),
+            dma((2 * SQUARES,)), dma((2 * SQUARES,)), dma((3,)), dma((3,)),
+            dma((3,)), dma((3,)), dma((3,)), dma((3,)), dma, dma,
+            dma((6,)), dma((6,)), dma((NP - 1,)), dma((NP - 1,)), dma((7,)), dma((7,)),
         ],
         compiler_params=pltpu.CompilerParams(
             collective_id=1, has_side_effects=True, vmem_limit_bytes=60 * 1024 * 1024

time: 102 us -> 97.8 us (0.959)
  Pallas kernels: 101 us -> 97 us
    pallas_call x1, Pallas kernels: 44.5 us -> 40.5 us  [collect(): pl.pallas_call(collect_kernel, out_shape=(jax.ShapeDtypeStruct((SLOTS, D)...]
where the time goes in v3:
time: 97.8 us; the launch traced here: 97.6 us
  Pallas kernels  97 us (99%)
    pallas_call x1, Pallas kernels, collect(): pl.pallas_call(collect_kernel, out_shape=(jax.ShapeDtypeStruct((SLOTS, D)...  40.5 us
    pallas_call x1, Pallas kernels, deliver(): pl.pallas_call(deliver_kernel, out_shape=(jax.ShapeDtypeStruct((PADDED, D...  28 us
    pallas_call x1, Pallas kernels, layer(): pl.pallas_call(layer_kernel, grid=(TILES,), out_shape=(by_edge, by_cell,...  25.8 us
    pallas_call x1, Pallas kernels, finish(): pl.pallas_call(finish_kernel, out_shape=(jax.ShapeDtypeStruct((C, D), BF)...  2.69 us

profile of v3, /device:TPU:1, one launch (start us, length us, event | category | flops | bytes accessed | tf_op | source)
XLA Modules:
  0.0 97.6 jit_solution(4064253880752469323)
XLA Ops:
  0.6 28.0 %deliver.1 = (bf16[640,512]{1,0:T(8,128)(2,1)}, f32[16,128]{1,0:T(8,128)}, s32[1,512]{1,0:T(1,128)}) custom-call(bf16[512,512]{1,0:T(8,128)(2,1)} %bitcast.12, s32[1,512]{1,0:T(1,128)} %tgt_ref.1), custom_call_target="tpu_custom_call" | custom-call | tf_op jit(solution)/shard_map/deliver/pallas_call | solution.py:144
  28.7 25.8 %layer.1 = (bf16[2048,512]{1,0:T(8,128)(2,1)}, bf16[512,512]{1,0:T(8,128)(2,1)}, bf16[2048,512]{1,0:T(8,128)(2,1)}, f32[512,512]{1,0:T(8,128)}, bf16[2,64,512]{2...) custom-call(bf16[640,512]{1,0:T(8,128)(2,1)} %get-tuple-element.26.p, ...), custom_call_target="tpu_custom_call" | custom-call | tf_op jit(solution)/shard_map/layer/pallas_call | solution.py:278
  54.5 40.5 %collect.1 = (bf16[768,512]{1,0:T(8,128)(2,1)}, bf16[224,512]{1,0:T(8,128)(2,1)}) custom-call(f32[512,512]{1,0:T(8,128)} %get-tuple-element.29.ng_ref, bf16[2,64,512]{2,1,0:T(8,128)(2,1)} %get-tuple-element.30.halo_ref, f32[16,128]{1,0:T(8,128)} %get-tuple-element.31.ids_ref, bf16[2048,512]{1,0:T(8,128)(2,1)} %bitcast.9, ...), custom_call_target="tpu_custom_call" | custom-call | tf_op jit(solution)/shard_map/collect/pallas_call | solution.py:579
  94.9 2.7 %finish.1 = (bf16[512,512]{1,0:T(8,128)(2,1)}, f32[224,512]{1,0:T(8,128)}) custom-call(bf16[768,512]{1,0:T(8,128)(2,1)} %get-tuple-element.41.back_ref, s32[1,512]{1,0:T(1,128)} %get-tuple-element.42.slot_ref, bf16[224,512]{1,0:T(8,128)(2,1)} %get-tuple-element.43.fin_ref), custom_call_target="tpu_custom_call" | custom-call | tf_op jit(solution)/shard_map/finish/pallas_call | solution.py:566

commit v4 on v3

--- a/solution.py
+++ b/solution.py
@@ -75,9 +75,10 @@
 
 
 def deliver_kernel(
-    h_ref, tgt_ref, pad_ref, ids_ref, slot_ref,
-    sbuf, rbuf, sids, rids, edge_out, edge_in, mt,
-    send, recv, isend, irecv, hsend, hrecv,
+    h_hbm, tgt_hbm, src_hbm, edges_hbm, w_hbm,
+    pad_ref, ids_ref, slot_ref, sel_ref, self_ref,
+    h_ref, tgt_ref, src_ref, edges, w_self, sbuf, rbuf, sids, rids, edge_out, edge_in, mt,
+    send, recv, isend, irecv, hsend, hrecv, lsem,
 ):
     geom = lax.axis_index("geom")
     me = lax.axis_index("dom")
@@ -85,6 +86,15 @@
     for p in range(1, NP):
         signal(barrier, geom, (me + p) % NP)
 
+    loads = [
+        pltpu.make_async_copy(far, near, lsem.at[n])
+        for n, (far, near) in enumerate(
+            ((tgt_hbm, tgt_ref), (h_hbm, h_ref), (edges_hbm, edges), (w_hbm.at[0:D], w_self), (src_hbm, src_ref))
+        )
+    ]
+    for load in loads:
+        load.start()
+    loads[0].wait()
     tgt = tgt_ref[...]
     off = ((tgt >> 9) - me) & (NP - 1)
     row = tgt & (C - 1)
@@ -101,6 +111,7 @@
     ids = 32.0 * coded[0:NP] + coded[NP : 2 * NP] + coded[2 * NP :] - 1.0
     for p in range(NP):
         sids[p] = jnp.broadcast_to(ids[p : p + 1, :], (8, 128))
+    loads[1].wait()
     packed = nn(pack_matrix(slot), h_ref[...]).astype(BF)
     sbuf[...] = packed.reshape(NP, CAP, D)
     rbuf[0] = packed[0:CAP]
@@ -113,6 +124,15 @@
         copies.append(remote(sbuf.at[p], rbuf.at[p], send.at[p], recv.at[p], geom, peer))
     for copy in copies:
         copy.start()
+    for load in loads[2:]:
+        load.wait()
+    for t in range(TILES):
+        rows = slice(t * TE, (t + 1) * TE)
+        src = src_ref[:, rows] - (me * C - HB)
+        src_col = jnp.broadcast_to(src.astype(F32), (128, TE)).T.astype(jnp.int32)
+        for b in range(PADDED // 128):
+            sel_ref[rows, b * 128 : (b + 1) * 128] = (src_col == iota((TE, 128), 1) + b * 128).astype(BF)
+        self_ref[rows, :] = nn(edges[rows, :], w_self[...]).astype(BF)
     for copy in copies[0::2]:
         copy.wait_recv()
     got = jnp.concatenate([ids[0:1]] + [rids[p, 0:1, :] for p in range(1, NP)], axis=0)
@@ -139,18 +159,26 @@
     to_next.wait_send()
 
 
-def deliver(h, tgt):
+def deliver(h, tgt, source, edges, wei):
     vm = pl.BlockSpec(memory_space=pltpu.VMEM)
+    hbm = pl.BlockSpec(memory_space=pltpu.HBM)
     return pl.pallas_call(
         deliver_kernel,
         out_shape=(
             jax.ShapeDtypeStruct((PADDED, D), BF),
             jax.ShapeDtypeStruct((NP, 128), F32),
             jax.ShapeDtypeStruct((1, C), jnp.int32),
-        ),
-        in_specs=[vm, vm],
-        out_specs=(vm, vm, vm),
+            jax.ShapeDtypeStruct((C * K, PADDED), BF),
+            jax.ShapeDtypeStruct((C * K, D), BF),
+        ),
+        in_specs=[hbm] * 5,
+        out_specs=(vm,) * 5,
         scratch_shapes=[
+            pltpu.VMEM((C, D), BF),
+            pltpu.VMEM((1, C), jnp.int32),
+            pltpu.VMEM((1, C * K), jnp.int32),
+            pltpu.VMEM((C * K, D), BF),
+            pltpu.VMEM((D, D), BF),
             pltpu.VMEM((NP, CAP, D), BF),
             pltpu.VMEM((NP, CAP, D), BF),
             pltpu.VMEM((NP, 8, 128), F32),
@@ -160,17 +188,21 @@
             pltpu.VMEM((SLOTS, C), BF),
         ]
         + [pltpu.SemaphoreType.DMA((NP,))] * 4
-        + [pltpu.SemaphoreType.DMA((2,))] * 2,
-        compiler_params=pltpu.CompilerParams(collective_id=0, has_side_effects=True),
+        + [pltpu.SemaphoreType.DMA((2,))] * 2
+        + [pltpu.SemaphoreType.DMA((5,))],
+        compiler_params=pltpu.CompilerParams(
+            collective_id=0, has_side_effects=True, vmem_limit_bytes=18 * 1024 * 1024
+        ),
+        cost_estimate=pl.CostEstimate(flops=20_000_000_000, bytes_accessed=60_000_000, transcendentals=0),
         name="deliver",
-    )(h, tgt)
+    )(*(pltpu.with_memory_space_constraint(a, pltpu.HBM) for a in (h, tgt, source, edges, wei)))
 
 
 def layer_kernel(
-    pad_ref, src_ref, edges_ref, cotn_ref, cote_ref, wei_ref, weo_ref, wni_ref, wno_ref,
+    pad_ref, src_ref, sel_ref, self_ref, edges_ref, cotn_ref, cote_ref, wei_ref, weo_ref, wni_ref, wno_ref,
     edge_new_ref, node_new_ref, grad_edge_ref, ng_ref, halo_ref,
     hid, post_grad, pre_grad, summed_ref, node_hid_ref, node_pre_ref, node_post_ref, recv_ref, send_ref,
-    sel, sel_t, comb, big, slope, normed, inv, ups, total,
+    spread, four, comb, big, slope, normed, inv, ups, total,
 ):
     step = pl.program_id(0)
     me = lax.axis_index("dom")
@@ -181,20 +213,14 @@
     @pl.when(step == 0)
     def _():
         comb[0:PADDED, :] = nn(pad_ref[...], w_send[...]).astype(BF)
-        sel[:, PADDED:] = (iota((TE, TC), 0) // K == iota((TE, TC), 1)).astype(BF)
-        sel_t[PADDED:, :] = (iota((TC, TE), 1) // K == iota((TC, TE), 0)).astype(BF)
+        spread[...] = (iota((TE, TC), 0) // K == iota((TE, TC), 1)).astype(BF)
+        four[...] = (iota((TC, TE), 1) // K == iota((TC, TE), 0)).astype(BF)
         total[...] = jnp.zeros_like(total)
 
     nodes = pad_ref[pl.ds(pl.multiple_of(HB + step * TC, HB), TC), :]
-    edges = edges_ref[...]
-    src = src_ref[...] - (me * C - HB)
-    sel_t[0:PADDED, :] = (iota((PADDED, TE), 0) == src).astype(BF)
-    src_col = jnp.broadcast_to(src.astype(F32), (128, TE)).T.astype(jnp.int32)
-    for b in range(PADDED // 128):
-        sel[:, b * 128 : (b + 1) * 128] = (src_col == iota((TE, 128), 1) + b * 128).astype(BF)
     comb[PADDED:, :] = nn(nodes, w_recv[...]).astype(BF)
 
-    big[...] = nn(edges, w_self[...]) + nn(sel[...], comb[...])
+    big[...] = self_ref[...].astype(F32) + nn(jnp.concatenate([sel_ref[...], spread[...]], axis=1), comb[...])
     for r in range(0, TE, RC):
         v = big[r : r + RC, :]
         s = sigmoid(v)
@@ -211,10 +237,9 @@
         inv[r : r + RC, :] = jnp.broadcast_to(i, (RC, 128))
         edge_new_ref[r : r + RC, :] = (edges_ref[r : r + RC, :].astype(F32) + n).astype(BF)
 
-    four = sel_t[PADDED:, :]
-    summed = nn(four, edge_new_ref[...]).astype(BF)
+    summed = nn(four[...], edge_new_ref[...]).astype(BF)
     summed_ref[...] = summed
-    v = nn(nodes, w_nself[...]) + nn(summed, w_nagg[...])
+    v = nn(jnp.concatenate([nodes, summed], axis=1), wni_ref[...])
     s = sigmoid(v)
     h = v * s
     node_slope = s + h * (1.0 - s)
@@ -234,7 +259,7 @@
     node_pre_ref[...] = node_pre_grad
     spread_grad = nt(node_pre_grad, w_nagg[...]).astype(BF)
 
-    ups[...] = nn(sel[:, PADDED:], spread_grad)
+    ups[...] = nn(spread[...], spread_grad)
     for r in range(0, TE, RC):
         u = cote_ref[r : r + RC, :].astype(F32) + ups[r : r + RC, :]
         ups[r : r + RC, :] = u
@@ -249,8 +274,11 @@
     big[...] = nt(g, w_self[...])
     for r in range(0, TE, RC):
         grad_edge_ref[r : r + RC, :] = (ups[r : r + RC, :] + big[r : r + RC, :]).astype(BF)
-    total[...] += nn(sel_t[0:PADDED, :], g)
-    recv_grad = nn(four, g).astype(BF)
+    src = src_ref[...] - (me * C - HB)
+    sel_t = (iota((PADDED, TE), 0) == src).astype(BF)
+    gathered = nn(jnp.concatenate([sel_t, four[...]], axis=0), g)
+    total[...] += gathered[0:PADDED]
+    recv_grad = gathered[PADDED:].astype(BF)
     recv_ref[...] = recv_grad
     ng_ref[rows, :] = (
         cotn_ref[...].astype(F32) + nt(node_pre_grad, w_nself[...]) + nt(recv_grad, w_recv[...])
@@ -266,7 +294,7 @@
         halo_ref[1] = back[HB + C :].astype(BF)
 
 
-def layer(padded, source, edges, cot_nodes, cot_edges, wei, weo, wni, wno):
+def layer(padded, source, sel, pre_self, edges, cot_nodes, cot_edges, wei, weo, wni, wno):
     def whole(shape):
         return pl.BlockSpec(shape, lambda i: (0,) * len(shape), pipeline_mode=pl.Buffered(1))
 
@@ -288,6 +316,8 @@
         in_specs=[
             whole((PADDED, D)),
             pl.BlockSpec((1, TE), lambda i: (0, i)),
+            pl.BlockSpec((TE, PADDED), lambda i: (i, 0)),
+            tile(TE),
             tile(TE), tile(TC), tile(TE),
             whole((3 * D, D)), whole((D, D)), whole((2 * D, D)), whole((D, D)),
         ],
@@ -298,8 +328,8 @@
             whole((PADDED, D)),
         ),
         scratch_shapes=[
-            pltpu.VMEM((TE, SEL), BF),
-            pltpu.VMEM((SEL, TE), BF),
+            pltpu.VMEM((TE, TC), BF),
+            pltpu.VMEM((TC, TE), BF),
             pltpu.VMEM((SEL, D), BF),
             pltpu.VMEM((TE, D), F32),
             pltpu.VMEM((TE, D), F32),
@@ -308,9 +338,10 @@
             pltpu.VMEM((TE, D), F32),
             pltpu.VMEM((PADDED, D), F32),
         ],
-        compiler_params=pltpu.CompilerParams(vmem_limit_bytes=60 * 1024 * 1024),
+        compiler_params=pltpu.CompilerParams(vmem_limit_bytes=30 * 1024 * 1024),
+        cost_estimate=pl.CostEstimate(flops=20_000_000_000, bytes_accessed=40_000_000, transcendentals=4_000_000),
         name="layer",
-    )(padded, source, edges, cot_nodes, cot_edges, wei, weo, wni, wno)
+    )(padded, source, sel, pre_self, edges, cot_nodes, cot_edges, wei, weo, wni, wno)
 
 
 ROWS = SQUARES * D
@@ -323,11 +354,10 @@
 
 def collect_kernel(
     ng_ref, halo_ref, ids_ref,
-    edges_hbm, pad_hbm, hid_hbm, post_hbm, pre_hbm, summed_hbm, nhid_hbm, npre_hbm, npost_hbm, recv_hbm, send_hbm,
+    edges, pad, hid, post, pre, summed, nhid, npre, npost, recv_g, send_g,
     back_ref, fin_ref,
-    edges, pad, hid, post, pre, summed, nhid, npre, npost, recv_g, send_g,
     hbuf, sback, rback, wown, wsend, pbuf, wsum, r1, p1, r2, r3, fin, wx, rx, px, ri, ag,
-    lsem, hsend, hrecv, bsend, brecv, psend, precv, s1, v1, s2, v2, s3, v3, s4, v4, sx, vx, si, vi, sg, vg,
+    hsend, hrecv, bsend, brecv, psend, precv, s1, v1, s2, v2, s3, v3, s4, v4, sx, vx, si, vi, sg, vg,
 ):
     geom = lax.axis_index("geom")
     me = lax.axis_index("dom")
@@ -350,20 +380,6 @@
         signal(barrier, (geom + d) % 8, me)
         signals += 1
 
-    pairs = (
-        (npre_hbm, npre), (pad_hbm, pad), (summed_hbm, summed), (npost_hbm, npost), (nhid_hbm, nhid),
-        (post_hbm, post), (hid_hbm, hid), (recv_hbm, recv_g), (send_hbm, send_g), (pre_hbm, pre), (edges_hbm, edges),
-    )
-    loads = {}
-    for n, (far, near) in enumerate(pairs):
-        loads[id(near)] = pltpu.make_async_copy(far, near, lsem.at[n])
-        loads[id(near)].start()
-
-    def ready(*refs):
-        for ref in refs:
-            if id(ref) in loads:
-                loads.pop(id(ref)).wait()
-
     scale = 1.0 / math.sqrt(8 * NP * C * K)
     inner = slice(HB, HB + C)
     operands = {
@@ -374,7 +390,6 @@
 
     def square(q):
         left, cut, right = operands[q]
-        ready(left, right)
         rows = left[...] if cut is None else left[cut, :]
         value = (tn(rows, right[...]) * scale).astype(BF)
         for c in range(2):
@@ -568,13 +583,13 @@
         out_shape=(jax.ShapeDtypeStruct((C, D), BF), jax.ShapeDtypeStruct((PER_DOM, D), F32)),
         in_specs=[vm] * 3,
         out_specs=(vm, vm),
+        compiler_params=pltpu.CompilerParams(vmem_limit_bytes=8 * 1024 * 1024),
         name="finish",
     )(back, slot, fin)
 
 
 def collect(ng, halo, ids, *operands):
     vm = pl.BlockSpec(memory_space=pltpu.VMEM)
-    hbm = pl.BlockSpec(memory_space=pl.ANY)
     dma = pltpu.SemaphoreType.DMA
     return pl.pallas_call(
         collect_kernel,
@@ -582,10 +597,9 @@
             jax.ShapeDtypeStruct((SLOTS, D), BF),
             jax.ShapeDtypeStruct((PER_DOM, D), BF),
         ),
-        in_specs=[vm] * 3 + [hbm] * len(operands),
+        in_specs=[vm] * (3 + len(operands)),
         out_specs=(vm, vm),
-        scratch_shapes=[pltpu.VMEM(a.shape, a.dtype) for a in operands]
-        + [
+        scratch_shapes=[
             pltpu.VMEM((2, HB, D), BF),
             pltpu.VMEM((NP, CAP, D), BF),
             pltpu.VMEM((NP, CAP, D), BF),
@@ -603,13 +617,13 @@
             pltpu.VMEM((NP, PART, QW), BF),
             pltpu.VMEM((NP - 1, PART, QW), BF),
             pltpu.VMEM((8, PART, QW), BF),
-            dma((len(operands),)), dma((2,)), dma((2,)), dma((NP,)), dma((NP,)),
+            dma((2,)), dma((2,)), dma((NP,)), dma((NP,)),
             dma((2 * SQUARES,)), dma((2 * SQUARES,)), dma((3,)), dma((3,)),
             dma((3,)), dma((3,)), dma((3,)), dma((3,)), dma, dma,
             dma((6,)), dma((6,)), dma((NP - 1,)), dma((NP - 1,)), dma((7,)), dma((7,)),
         ],
         compiler_params=pltpu.CompilerParams(
-            collective_id=1, has_side_effects=True, vmem_limit_bytes=60 * 1024 * 1024
+            collective_id=1, has_side_effects=True, vmem_limit_bytes=32 * 1024 * 1024
         ),
         name="collect",
     )(ng, halo, ids, *operands)
@@ -618,9 +632,9 @@
 def local(
     h_in, edge_in, new_index, source, w_edge_in, w_edge_out, w_node_in, w_node_out, cot_nodes, cot_edges
 ):
-    padded, ids, slot = deliver(h_in[0], new_index)
+    padded, ids, slot, sel, pre_self = deliver(h_in[0], new_index, source, edge_in[0], w_edge_in)
     edge_new, node_new, grad_edge, ng, halo, hid, post, pre, summed, nhid, npre, npost, recv, send = layer(
-        padded, source, edge_in[0], cot_nodes[0], cot_edges[0], w_edge_in, w_edge_out, w_node_in, w_node_out
+        padded, source, sel, pre_self, edge_in[0], cot_nodes[0], cot_edges[0], w_edge_in, w_edge_out, w_node_in, w_node_out
     )
     back, fin = collect(
         ng, halo, ids, edge_in[0], padded, hid, post, pre, summed, nhid, npre, npost, recv, send

time: 97.8 us -> 86.9 us (0.89)
  Pallas kernels: 97 us -> 86 us
    pallas_call x1, Pallas kernels: 25.8 us -> 19.9 us  [layer(): pl.pallas_call(layer_kernel, grid=(TILES,), out_shape=(by_edge, by_cell,...]
    pallas_call x1, Pallas kernels: 40.5 us -> 38.5 us  [collect(): pl.pallas_call(collect_kernel, out_shape=(jax.ShapeDtypeStruct((SLOTS, D)...]
    pallas_call x1, Pallas kernels: 28 us -> 26.1 us  [deliver(): pl.pallas_call(deliver_kernel, out_shape=(jax.ShapeDtypeStruct((PADDED, D...]
    pallas_call x1, Pallas kernels: 2.69 us -> 1.51 us  [finish(): pl.pallas_call(finish_kernel, out_shape=(jax.ShapeDtypeStruct((C, D), BF)...]
where the time goes in v4:
time: 86.9 us; the launch traced here: 86.8 us
  Pallas kernels  86 us (99%)
    pallas_call x1, Pallas kernels, collect(): pl.pallas_call(collect_kernel, out_shape=(jax.ShapeDtypeStruct((SLOTS, D)...  38.5 us
    pallas_call x1, Pallas kernels, deliver(): pl.pallas_call(deliver_kernel, out_shape=(jax.ShapeDtypeStruct((PADDED, D...  26.1 us
    pallas_call x1, Pallas kernels, layer(): pl.pallas_call(layer_kernel, grid=(TILES,), out_shape=(by_edge, by_cell,...  19.9 us

profile of v4, /device:TPU:1, one launch (start us, length us, event | category | flops | bytes accessed | tf_op | source)
XLA Modules:
  0.0 86.8 jit_solution(4383652289235587155)
XLA Ops:
  0.6 0.0 copy-start
  0.6 0.0 copy-start.1
  0.7 0.0 copy-start.2
  0.7 0.0 copy-start.3
  0.7 0.0 copy-start.4
  0.7 0.0 copy-start.5
  0.7 0.0 copy-start.6
  0.7 0.0 copy-start.7
  0.7 26.1 %deliver.1 = (bf16[640,512]{1,0:T(8,128)(2,1)S(1)}, f32[16,128]{1,0:T(8,128)S(1)}, s32[1,512]{1,0:T(1,128)S(1)}, bf16[2048,640]{1,0:T(8,128)(2,1)S(1)}, bf16[2048,512]{1,0:T(8,128)(2,1)S(1)}) custom-call(bf16[512,512]{1,0:T(8,128)(2,1)} %bitcast.13, s32[1,512]{1,0:T(1,128)} %tgt_hbm.1, s32[1,2048]{1,0:T(1,128)} %src_ref.1, bf16[2048,512]{1,0:T(8,128)(2,1)} %bitcast.8, ...), custom_call_target="tpu_custom_call" | custom-call | flops 20000000000 | bytes 60000000 | tf_op jit(solution)/shard_map/deliver/pallas_call | solution.py:165
  26.8 0.0 copy-done
  26.8 0.0 copy-done.1
  26.9 0.0 copy-done.2
  26.9 0.0 copy-done.3
  26.9 0.0 copy-done.4
  26.9 0.0 copy-done.5
  26.9 0.0 copy-done.6
  26.9 0.0 copy-done.7
  26.9 19.9 %layer.1 = (bf16[2048,512]{1,0:T(8,128)(2,1)}, bf16[512,512]{1,0:T(8,128)(2,1)}, bf16[2048,512]{1,0:T(8,128)(2,1)}, f32[512,512]{1,0:T(8,128)S(1)}, bf16[2,64,51...) custom-call(bf16[640,512]{1,0:T(8,128)(2,1)S(1)} %get-tuple-element., ...), custom_call_target="tpu_custom_call" | custom-call | flops 20000000000 | bytes 40000000 | tf_op jit(solution)/shard_map/layer/pallas_call | solution.py:306
  46.8 38.5 %collect.1 = (bf16[768,512]{1,0:T(8,128)(2,1)S(1)}, bf16[224,512]{1,0:T(8,128)(2,1)S(1)}) custom-call(f32[512,512]{1,0:T(8,128)S(1)} %get-tuple-element.33.ng_ref, bf16[2,64,512]{2,1,0:T(8,128)(2,1)S(1)} %get-tuple-element.34.halo_ref, f32[16,128]{1,0:T(8,128)S(1)} %get-tuple-element.35.ids_ref, bf16[2048,512]{1,0:T(8,128)(2,1)S(1)} %bitcast.10, ...), custom_call_target="tpu_custom_call" | custom-call | tf_op jit(solution)/shard_map/collect/pallas_call | solution.py:594
  85.3 1.5 %finish.1 = (bf16[512,512]{1,0:T(8,128)(2,1)}, f32[224,512]{1,0:T(8,128)}) custom-call(bf16[768,512]{1,0:T(8,128)(2,1)S(1)} %get-tuple-element.45.back_ref, s32[1,512]{1,0:T(1,128)S(1)} %get-tuple-element.46.slot_ref, bf16[224,512]{1,0:T(8,128)(2,1)S(1)} %get-tuple-element.47.fin_ref), custom_call_target="tpu_custom_call" | custom-call | tf_op jit(solution)/shard_map/finish/pallas_call | solution.py:581
Async XLA Ops:
  0.6 26.2 %copy-start = (bf16[1,2048,512]{2,1,0:T(8,128)(2,1)S(1)}, bf16[1,2048,512]{2,1,0:T(8,128)(2,1)}, u32[]{:S(2)}) copy-start(bf16[1,2048,512]{2,1,0:T(8,128)(2,1)} %param.11) | copy-start | bytes 6291460
  0.6 26.2 %copy-start.1 = (bf16[1,2048,512]{2,1,0:T(8,128)(2,1)S(1)}, bf16[1,2048,512]{2,1,0:T(8,128)(2,1)}, u32[]{:S(2)}) copy-start(bf16[1,2048,512]{2,1,0:T(8,128)(2,1)} %param.19) | copy-start | bytes 6291460
  0.7 26.2 %copy-start.2 = (bf16[1536,512]{1,0:T(8,128)(2,1)S(1)}, bf16[1536,512]{1,0:T(8,128)(2,1)}, u32[]{:S(2)}) copy-start(bf16[1536,512]{1,0:T(8,128)(2,1)} %wei_ref.1) | copy-start | bytes 4718596
  0.7 26.2 %copy-start.3 = (bf16[1024,512]{1,0:T(8,128)(2,1)S(1)}, bf16[1024,512]{1,0:T(8,128)(2,1)}, u32[]{:S(2)}) copy-start(bf16[1024,512]{1,0:T(8,128)(2,1)} %wni_ref.1) | copy-start | bytes 3145732
  0.7 26.2 %copy-start.4 = (bf16[1,512,512]{2,1,0:T(8,128)(2,1)S(1)}, bf16[1,512,512]{2,1,0:T(8,128)(2,1)}, u32[]{:S(2)}) copy-start(bf16[1,512,512]{2,1,0:T(8,128)(2,1)} %param.18) | copy-start | bytes 1572868
  0.7 26.2 %copy-start.5 = (bf16[512,512]{1,0:T(8,128)(2,1)S(1)}, bf16[512,512]{1,0:T(8,128)(2,1)}, u32[]{:S(2)}) copy-start(bf16[512,512]{1,0:T(8,128)(2,1)} %weo_ref.1) | copy-start | bytes 1572868
  0.7 26.2 %copy-start.6 = (bf16[512,512]{1,0:T(8,128)(2,1)S(1)}, bf16[512,512]{1,0:T(8,128)(2,1)}, u32[]{:S(2)}) copy-start(bf16[512,512]{1,0:T(8,128)(2,1)} %wno_ref.1) | copy-start | bytes 1572868
  0.7 26.2 %copy-start.7 = (s32[1,2048]{1,0:T(1,128)S(1)}, s32[1,2048]{1,0:T(1,128)}, u32[]{:S(2)}) copy-start(s32[1,2048]{1,0:T(1,128)} %src_ref.1) | copy-start | bytes 24580

commit v5 on v4

--- a/solution.py
+++ b/solution.py
@@ -199,9 +199,9 @@
 
 
 def layer_kernel(
-    pad_ref, src_ref, sel_ref, self_ref, edges_ref, cotn_ref, cote_ref, wei_ref, weo_ref, wni_ref, wno_ref,
+    pad_ref, src_all, sel_all, self_all, edges_all, cotn_all, cote_all, wei_ref, weo_ref, wni_ref, wno_ref,
     edge_new_ref, node_new_ref, grad_edge_ref, ng_ref, halo_ref,
-    hid, post_grad, pre_grad, summed_ref, node_hid_ref, node_pre_ref, node_post_ref, recv_ref, send_ref,
+    hid_all, post_all, pre_all, summed_all, node_hid_all, node_pre_all, node_post_all, recv_all, send_ref,
     spread, four, comb, big, slope, normed, inv, ups, total,
 ):
     step = pl.program_id(0)
@@ -209,6 +209,12 @@
     w_self, w_send, w_recv = wei_ref.at[0:D], wei_ref.at[D : 2 * D], wei_ref.at[2 * D : 3 * D]
     w_nself, w_nagg = wni_ref.at[0:D], wni_ref.at[D : 2 * D]
     rows = pl.ds(pl.multiple_of(step * TC, TC), TC)
+    lines = pl.ds(pl.multiple_of(step * TE, TE), TE)
+    sel_ref, self_ref, edges_ref, cote_ref = (ref.at[lines] for ref in (sel_all, self_all, edges_all, cote_all))
+    hid, post_grad, pre_grad = (ref.at[lines] for ref in (hid_all, post_all, pre_all))
+    cotn_ref, summed_ref, node_hid_ref, node_pre_ref, node_post_ref, recv_ref = (
+        ref.at[rows] for ref in (cotn_all, summed_all, node_hid_all, node_pre_all, node_post_all, recv_all)
+    )
 
     @pl.when(step == 0)
     def _():
@@ -274,7 +280,7 @@
     big[...] = nt(g, w_self[...])
     for r in range(0, TE, RC):
         grad_edge_ref[r : r + RC, :] = (ups[r : r + RC, :] + big[r : r + RC, :]).astype(BF)
-    src = src_ref[...] - (me * C - HB)
+    src = src_all[:, lines] - (me * C - HB)
     sel_t = (iota((PADDED, TE), 0) == src).astype(BF)
     gathered = nn(jnp.concatenate([sel_t, four[...]], axis=0), g)
     total[...] += gathered[0:PADDED]
@@ -295,8 +301,7 @@
 
 
 def layer(padded, source, sel, pre_self, edges, cot_nodes, cot_edges, wei, weo, wni, wno):
-    def whole(shape):
-        return pl.BlockSpec(shape, lambda i: (0,) * len(shape), pipeline_mode=pl.Buffered(1))
+    vm = pl.BlockSpec(memory_space=pltpu.VMEM)
 
     def tile(rows):
         return pl.BlockSpec((rows, D), lambda i: (i, 0))
@@ -313,20 +318,8 @@
             by_edge, by_edge, by_edge, by_cell, by_cell, by_cell, by_cell, by_cell,
             jax.ShapeDtypeStruct((PADDED, D), BF),
         ),
-        in_specs=[
-            whole((PADDED, D)),
-            pl.BlockSpec((1, TE), lambda i: (0, i)),
-            pl.BlockSpec((TE, PADDED), lambda i: (i, 0)),
-            tile(TE),
-            tile(TE), tile(TC), tile(TE),
-            whole((3 * D, D)), whole((D, D)), whole((2 * D, D)), whole((D, D)),
-        ],
-        out_specs=(
-            tile(TE), tile(TC), tile(TE),
-            whole((C, D)), whole((2, HB, D)),
-            tile(TE), tile(TE), tile(TE), tile(TC), tile(TC), tile(TC), tile(TC), tile(TC),
-            whole((PADDED, D)),
-        ),
+        in_specs=[vm] * 11,
+        out_specs=(tile(TE), tile(TC), tile(TE)) + (vm,) * 11,
         scratch_shapes=[
             pltpu.VMEM((TE, TC), BF),
             pltpu.VMEM((TC, TE), BF),
@@ -507,7 +500,7 @@
             for q in squares:
                 pair[c, q].start()
 
-    for q in (4, 5, 6):
+    for q in (4, 5, 6, 3, 2, 1, 0):
         square(q)
     pl.semaphore_wait(barrier, signals)
     send_pairs(4, 5, 6)
@@ -515,12 +508,8 @@
     to_next = remote(halo_ref.at[1], hbuf.at[0], hsend.at[1], hrecv.at[0], geom, (me + 1) % NP)
     to_prev.start()
     to_next.start()
-    square(3)
-    send_pairs(3)
+    send_pairs(3, 2, 1, 0)
     join_x(1, EARLY, NP, (4, 5, 6))
-    for q in (2, 1, 0):
-        square(q)
-        send_pairs(q)
     join_x(1, 0, EARLY, range(SQUARES))
     join(0)
 
@@ -540,8 +529,8 @@
     for copy in backs:
         copy.start()
 
+    narrow()
     narrow_x()
-    narrow()
     across()
     narrow_dom()
     for copy in backs:

time: 86.9 us -> 87 us (level)
  no operation moved by 1% of the time
where the time goes in v5:
time: 87 us; the launch traced here: 86.9 us
  Pallas kernels  86.1 us (99%)
    pallas_call x1, Pallas kernels, collect(): pl.pallas_call(collect_kernel, out_shape=(jax.ShapeDtypeStruct((SLOTS, D)...  38.6 us
    pallas_call x1, Pallas kernels, deliver(): pl.pallas_call(deliver_kernel, out_shape=(jax.ShapeDtypeStruct((PADDED, D...  26.1 us
    pallas_call x1, Pallas kernels, layer(): pl.pallas_call(layer_kernel, grid=(TILES,), out_shape=(by_edge, by_cell,...  19.8 us

profile of v5, /device:TPU:1, one launch (start us, length us, event | category | flops | bytes accessed | tf_op | source)
XLA Modules:
  0.0 86.9 jit_solution(15372808162548728741)
XLA Ops:
  0.6 0.0 copy-start
  0.6 0.0 copy-start.1
  0.7 0.0 copy-start.2
  0.7 0.0 copy-start.3
  0.7 0.0 copy-start.4
  0.7 0.0 copy-start.5
  0.7 0.0 copy-start.6
  0.7 0.0 copy-start.7
  0.7 26.1 %deliver.1 = (bf16[640,512]{1,0:T(8,128)(2,1)S(1)}, f32[16,128]{1,0:T(8,128)S(1)}, s32[1,512]{1,0:T(1,128)S(1)}, bf16[2048,640]{1,0:T(8,128)(2,1)S(1)}, bf16[2048,512]{1,0:T(8,128)(2,1)S(1)}) custom-call(bf16[512,512]{1,0:T(8,128)(2,1)} %bitcast.13, s32[1,512]{1,0:T(1,128)} %tgt_hbm.1, s32[1,2048]{1,0:T(1,128)} %src_all.1, bf16[2048,512]{1,0:T(8,128)(2,1)} %bitcast.8, ...), custom_call_target="tpu_custom_call" | custom-call | flops 20000000000 | bytes 60000000 | tf_op jit(solution)/shard_map/deliver/pallas_call | solution.py:165
  26.8 0.0 copy-done
  26.8 0.0 copy-done.1
  26.9 0.0 copy-done.2
  26.9 0.0 copy-done.3
  26.9 0.0 copy-done.4
  26.9 0.0 copy-done.5
  26.9 0.0 copy-done.6
  26.9 0.0 copy-done.7
  26.9 19.8 %layer.1 = (bf16[2048,512]{1,0:T(8,128)(2,1)}, bf16[512,512]{1,0:T(8,128)(2,1)}, bf16[2048,512]{1,0:T(8,128)(2,1)}, f32[512,512]{1,0:T(8,128)S(1)}, bf16[2,64,51...) custom-call(bf16[640,512]{1,0:T(8,128)(2,1)S(1)} %get-tuple-element., ...), custom_call_target="tpu_custom_call" | custom-call | flops 20000000000 | bytes 40000000 | tf_op jit(solution)/shard_map/layer/pallas_call | solution.py:311
  46.7 38.6 %collect.1 = (bf16[768,512]{1,0:T(8,128)(2,1)S(1)}, bf16[224,512]{1,0:T(8,128)(2,1)S(1)}) custom-call(f32[512,512]{1,0:T(8,128)S(1)} %get-tuple-element.33.ng_ref, bf16[2,64,512]{2,1,0:T(8,128)(2,1)S(1)} %get-tuple-element.34.halo_ref, f32[16,128]{1,0:T(8,128)S(1)} %get-tuple-element.35.ids_ref, bf16[2048,512]{1,0:T(8,128)(2,1)S(1)} %bitcast.10, ...), custom_call_target="tpu_custom_call" | custom-call | tf_op jit(solution)/shard_map/collect/pallas_call | solution.py:583
  85.4 1.5 %finish.1 = (bf16[512,512]{1,0:T(8,128)(2,1)}, f32[224,512]{1,0:T(8,128)}) custom-call(bf16[768,512]{1,0:T(8,128)(2,1)S(1)} %get-tuple-element.45.back_ref, s32[1,512]{1,0:T(1,128)S(1)} %get-tuple-element.46.slot_ref, bf16[224,512]{1,0:T(8,128)(2,1)S(1)} %get-tuple-element.47.fin_ref), custom_call_target="tpu_custom_call" | custom-call | tf_op jit(solution)/shard_map/finish/pallas_call | solution.py:570
Async XLA Ops:
  0.6 26.2 %copy-start = (bf16[1,2048,512]{2,1,0:T(8,128)(2,1)S(1)}, bf16[1,2048,512]{2,1,0:T(8,128)(2,1)}, u32[]{:S(2)}) copy-start(bf16[1,2048,512]{2,1,0:T(8,128)(2,1)} %param.11) | copy-start | bytes 6291460
  0.6 26.2 %copy-start.1 = (bf16[1,2048,512]{2,1,0:T(8,128)(2,1)S(1)}, bf16[1,2048,512]{2,1,0:T(8,128)(2,1)}, u32[]{:S(2)}) copy-start(bf16[1,2048,512]{2,1,0:T(8,128)(2,1)} %param.19) | copy-start | bytes 6291460
  0.7 26.2 %copy-start.2 = (bf16[1536,512]{1,0:T(8,128)(2,1)S(1)}, bf16[1536,512]{1,0:T(8,128)(2,1)}, u32[]{:S(2)}) copy-start(bf16[1536,512]{1,0:T(8,128)(2,1)} %wei_ref.1) | copy-start | bytes 4718596
  0.7 26.2 %copy-start.3 = (bf16[1024,512]{1,0:T(8,128)(2,1)S(1)}, bf16[1024,512]{1,0:T(8,128)(2,1)}, u32[]{:S(2)}) copy-start(bf16[1024,512]{1,0:T(8,128)(2,1)} %wni_ref.1) | copy-start | bytes 3145732
  0.7 26.2 %copy-start.4 = (bf16[1,512,512]{2,1,0:T(8,128)(2,1)S(1)}, bf16[1,512,512]{2,1,0:T(8,128)(2,1)}, u32[]{:S(2)}) copy-start(bf16[1,512,512]{2,1,0:T(8,128)(2,1)} %param.18) | copy-start | bytes 1572868
  0.7 26.2 %copy-start.5 = (bf16[512,512]{1,0:T(8,128)(2,1)S(1)}, bf16[512,512]{1,0:T(8,128)(2,1)}, u32[]{:S(2)}) copy-start(bf16[512,512]{1,0:T(8,128)(2,1)} %weo_ref.1) | copy-start | bytes 1572868
  0.7 26.2 %copy-start.6 = (bf16[512,512]{1,0:T(8,128)(2,1)S(1)}, bf16[512,512]{1,0:T(8,128)(2,1)}, u32[]{:S(2)}) copy-start(bf16[512,512]{1,0:T(8,128)(2,1)} %wno_ref.1) | copy-start | bytes 1572868
  0.7 26.2 %copy-start.7 = (s32[1,2048]{1,0:T(1,128)S(1)}, s32[1,2048]{1,0:T(1,128)}, u32[]{:S(2)}) copy-start(s32[1,2048]{1,0:T(1,128)} %src_all.1) | copy-start | bytes 24580

commit v6 on v5

--- a/solution.py
+++ b/solution.py
@@ -20,7 +20,7 @@
 NP = 16
 CAP = 48
 SLOTS = NP * CAP
-TC = 128
+TC = 256
 TE = TC * K
 TILES = C // TC
 SEL = PADDED + TC
@@ -141,14 +141,18 @@
         mt[pl.ds(p * CAP, CAP), :] = block
     for copy in copies[1::2]:
         copy.wait_recv()
-    nodes = tn(mt[...], rbuf[...].reshape(SLOTS, D)).astype(BF)
-    edge_out[0] = nodes[0:HB]
-    edge_out[1] = nodes[C - HB : C]
+    arrived = rbuf[...].reshape(SLOTS, D)
+    first = tn(mt[:, 0:128], arrived).astype(BF)
+    last = tn(mt[:, C - 128 : C], arrived).astype(BF)
+    edge_out[0] = first[0:HB]
+    edge_out[1] = last[128 - HB : 128]
     to_prev = remote(edge_out.at[0], edge_in.at[1], hsend.at[0], hrecv.at[1], geom, (me + NP - 1) % NP)
     to_next = remote(edge_out.at[1], edge_in.at[0], hsend.at[1], hrecv.at[0], geom, (me + 1) % NP)
     to_prev.start()
     to_next.start()
-    pad_ref[HB : HB + C, :] = nodes
+    pad_ref[HB : HB + 128, :] = first
+    pad_ref[HB + C - 128 : HB + C, :] = last
+    pad_ref[HB + 128 : HB + C - 128, :] = tn(mt[:, 128 : C - 128], arrived).astype(BF)
     to_prev.wait_recv()
     to_next.wait_recv()
     pad_ref[0:HB, :] = edge_in[0]

time: 87 us -> 84.3 us (0.969)
  Pallas kernels: 86.1 us -> 83.4 us
    pallas_call x1, Pallas kernels: 19.8 us -> 17.3 us  [layer(): pl.pallas_call(layer_kernel, grid=(TILES,), out_shape=(by_edge, by_cell,...]
where the time goes in v6:
time: 84.3 us; the launch traced here: 84.2 us
  Pallas kernels  83.4 us (99%)
    pallas_call x1, Pallas kernels, collect(): pl.pallas_call(collect_kernel, out_shape=(jax.ShapeDtypeStruct((SLOTS, D)...  38.7 us
    pallas_call x1, Pallas kernels, deliver(): pl.pallas_call(deliver_kernel, out_shape=(jax.ShapeDtypeStruct((PADDED, D...  26 us
    pallas_call x1, Pallas kernels, layer(): pl.pallas_call(layer_kernel, grid=(TILES,), out_shape=(by_edge, by_cell,...  17.3 us

profile of v6, /device:TPU:1, one launch (start us, length us, event | category | flops | bytes accessed | tf_op | source)
XLA Modules:
  0.0 84.2 jit_solution(17267389912715633838)
XLA Ops:
  0.6 0.0 copy-start
  0.6 0.0 copy-start.1
  0.7 0.0 copy-start.2
  0.7 0.0 copy-start.3
  0.7 0.0 copy-start.4
  0.7 0.0 copy-start.5
  0.7 0.0 copy-start.6
  0.7 0.0 copy-start.7
  0.7 26.0 %deliver.1 = (bf16[640,512]{1,0:T(8,128)(2,1)S(1)}, f32[16,128]{1,0:T(8,128)S(1)}, s32[1,512]{1,0:T(1,128)S(1)}, bf16[2048,640]{1,0:T(8,128)(2,1)S(1)}, bf16[2048,512]{1,0:T(8,128)(2,1)S(1)}) custom-call(bf16[512,512]{1,0:T(8,128)(2,1)} %bitcast.13, s32[1,512]{1,0:T(1,128)} %tgt_hbm.1, s32[1,2048]{1,0:T(1,128)} %src_all.1, bf16[2048,512]{1,0:T(8,128)(2,1)} %bitcast.8, ...), custom_call_target="tpu_custom_call" | custom-call | flops 20000000000 | bytes 60000000 | tf_op jit(solution)/shard_map/deliver/pallas_call | solution.py:169
  26.7 0.0 copy-done
  26.7 0.0 copy-done.1
  26.7 0.0 copy-done.2
  26.7 0.0 copy-done.3
  26.7 0.0 copy-done.4
  26.8 0.0 copy-done.5
  26.8 0.0 copy-done.6
  26.8 0.0 copy-done.7
  26.8 17.3 %layer.1 = (bf16[2048,512]{1,0:T(8,128)(2,1)}, bf16[512,512]{1,0:T(8,128)(2,1)}, bf16[2048,512]{1,0:T(8,128)(2,1)}, f32[512,512]{1,0:T(8,128)S(1)}, bf16[2,64,51...) custom-call(bf16[640,512]{1,0:T(8,128)(2,1)S(1)} %get-tuple-element., ...), custom_call_target="tpu_custom_call" | custom-call | flops 20000000000 | bytes 40000000 | tf_op jit(solution)/shard_map/layer/pallas_call | solution.py:315
  44.0 38.7 %collect.1 = (bf16[768,512]{1,0:T(8,128)(2,1)S(1)}, bf16[224,512]{1,0:T(8,128)(2,1)S(1)}) custom-call(f32[512,512]{1,0:T(8,128)S(1)} %get-tuple-element.33.ng_ref, bf16[2,64,512]{2,1,0:T(8,128)(2,1)S(1)} %get-tuple-element.34.halo_ref, f32[16,128]{1,0:T(8,128)S(1)} %get-tuple-element.35.ids_ref, bf16[2048,512]{1,0:T(8,128)(2,1)S(1)} %bitcast.10, ...), custom_call_target="tpu_custom_call" | custom-call | tf_op jit(solution)/shard_map/collect/pallas_call | solution.py:587
  82.7 1.5 %finish.1 = (bf16[512,512]{1,0:T(8,128)(2,1)}, f32[224,512]{1,0:T(8,128)}) custom-call(bf16[768,512]{1,0:T(8,128)(2,1)S(1)} %get-tuple-element.45.back_ref, s32[1,512]{1,0:T(1,128)S(1)} %get-tuple-element.46.slot_ref, bf16[224,512]{1,0:T(8,128)(2,1)S(1)} %get-tuple-element.47.fin_ref), custom_call_target="tpu_custom_call" | custom-call | tf_op jit(solution)/shard_map/finish/pallas_call | solution.py:574
Async XLA Ops:
  0.6 26.1 %copy-start = (bf16[1,2048,512]{2,1,0:T(8,128)(2,1)S(1)}, bf16[1,2048,512]{2,1,0:T(8,128)(2,1)}, u32[]{:S(2)}) copy-start(bf16[1,2048,512]{2,1,0:T(8,128)(2,1)} %param.11) | copy-start | bytes 6291460
  0.6 26.1 %copy-start.1 = (bf16[1,2048,512]{2,1,0:T(8,128)(2,1)S(1)}, bf16[1,2048,512]{2,1,0:T(8,128)(2,1)}, u32[]{:S(2)}) copy-start(bf16[1,2048,512]{2,1,0:T(8,128)(2,1)} %param.19) | copy-start | bytes 6291460
  0.7 26.1 %copy-start.2 = (bf16[1536,512]{1,0:T(8,128)(2,1)S(1)}, bf16[1536,512]{1,0:T(8,128)(2,1)}, u32[]{:S(2)}) copy-start(bf16[1536,512]{1,0:T(8,128)(2,1)} %wei_ref.1) | copy-start | bytes 4718596
  0.7 26.1 %copy-start.3 = (bf16[1024,512]{1,0:T(8,128)(2,1)S(1)}, bf16[1024,512]{1,0:T(8,128)(2,1)}, u32[]{:S(2)}) copy-start(bf16[1024,512]{1,0:T(8,128)(2,1)} %wni_ref.1) | copy-start | bytes 3145732
  0.7 26.1 %copy-start.4 = (bf16[1,512,512]{2,1,0:T(8,128)(2,1)S(1)}, bf16[1,512,512]{2,1,0:T(8,128)(2,1)}, u32[]{:S(2)}) copy-start(bf16[1,512,512]{2,1,0:T(8,128)(2,1)} %param.18) | copy-start | bytes 1572868
  0.7 26.1 %copy-start.5 = (bf16[512,512]{1,0:T(8,128)(2,1)S(1)}, bf16[512,512]{1,0:T(8,128)(2,1)}, u32[]{:S(2)}) copy-start(bf16[512,512]{1,0:T(8,128)(2,1)} %weo_ref.1) | copy-start | bytes 1572868
  0.7 26.1 %copy-start.6 = (bf16[512,512]{1,0:T(8,128)(2,1)S(1)}, bf16[512,512]{1,0:T(8,128)(2,1)}, u32[]{:S(2)}) copy-start(bf16[512,512]{1,0:T(8,128)(2,1)} %wno_ref.1) | copy-start | bytes 1572868
  0.7 26.1 %copy-start.7 = (s32[1,2048]{1,0:T(1,128)S(1)}, s32[1,2048]{1,0:T(1,128)}, u32[]{:S(2)}) copy-start(s32[1,2048]{1,0:T(1,128)} %src_all.1) | copy-start | bytes 24580
